TPU v7x, 512 devices: a whole 4x4x16 slice. The times are simulated.
512 devices in a mesh: lon: 32 (over z_lo, y), ch: 16 (over z_hi, x, core).
Axes of the slice: x: 4, y: 4, z: 16 (z_hi: 2, z_lo: 8; z = z_hi * 8 + z_lo), core: 2. Of those that a mesh axis runs over, the one named last changes fastest.
Arguments:
- features: bfloat16 [80, 480, 2048], P(None, 'lon', 'ch'), may hold values from -10 to 10
- pointwise_weight: bfloat16 [2048, 256], P('ch'), may hold values from -0.125 to 0.125
- w_atrous: bfloat16 [3, 3, 3, 2048, 256], P(None, None, None, 'ch'), may hold values from -0.046875 to 0.046875
- w_pool: bfloat16 [2048, 256], P('ch'), may hold values from -0.125 to 0.125
- w_proj: bfloat16 [1280, 256], replicated, may hold values from -0.15625 to 0.15625
- norm_gain: float32 [6, 256], replicated, may hold values from 0.1 to 1.9
- norm_shift: float32 [6, 256], replicated, may hold values from -3 to 3
Outputs:
- head_out: bfloat16 [80, 480, 256], P(None, 'lon', 'ch')
All inputs are finite; a program needn't handle non-finite values.
Results may differ from a plain program's by a relative error of at most 0.017.
Values may be sent and summed in bfloat16 or wider, within the bound.
A program may use at most 64 MiB of HBM per device.

v0:
```python
import jax
import jax.numpy as jnp
from jax import lax
from jax.sharding import PartitionSpec as P

BASE_DILATION = 12


def from_behind(value, axis, by):
    count = lax.axis_size(axis)
    return lax.ppermute(value, axis, [(i, (i + by) % count) for i in range(count)])


def branch_terms(padded, pointwise_weight, w_atrous, rows, cols, kernel_reach):
    centre = padded[kernel_reach : kernel_reach + rows, kernel_reach : kernel_reach + cols]
    chans = centre.shape[2]
    pixels = rows * cols
    terms = [
        jnp.dot(centre.reshape(pixels, chans), pointwise_weight, preferred_element_type=jnp.float32)
    ]
    for pyramid_level in range(3):
        step_stride = (pyramid_level + 1) * BASE_DILATION
        taps = []
        for row_off in range(3):
            for col_off in range(3):
                top = kernel_reach + (row_off - 1) * step_stride
                left = kernel_reach + (col_off - 1) * step_stride
                taps.append(padded[top : top + rows, left : left + cols])
        stacked = jnp.concatenate(taps, axis=2).reshape(pixels, 9 * chans)
        kernel = w_atrous[pyramid_level].reshape(9 * chans, w_atrous.shape[-1])
        terms.append(jnp.dot(stacked, kernel, preferred_element_type=jnp.float32))
    return jnp.stack(terms, axis=1)


def extend_columns(features, kernel_reach):
    cols = features.shape[1]
    hop_count = (kernel_reach + cols - 1) // cols
    west_parts = []
    east_parts = []
    for hop in range(1, hop_count + 1):
        needed = min(cols, kernel_reach - (hop - 1) * cols)
        west_parts.insert(0, from_behind(features[:, cols - needed :], "lon", hop))
        east_parts.append(from_behind(features[:, :needed], "lon", -hop))
    return jnp.concatenate(west_parts + [features] + east_parts, axis=1)


def local(features, pointwise_weight, w_atrous, w_pool, w_proj, norm_gain, norm_shift):
    rows, cols, chans = features.shape
    full = w_proj.shape[1]
    pixels = rows * cols
    kernel_reach = 3 * BASE_DILATION
    owned = full // lax.axis_size("ch")
    first = lax.axis_index("ch") * owned
    local_sum = jnp.sum(features, axis=(0, 1), dtype=jnp.float32)
    cells = pixels * lax.axis_size("lon")
    pool_weight = w_pool.astype(jnp.float32)
    column_total = lax.psum(local_sum, "lon")
    partial_pre = jnp.dot(column_total / cells, pool_weight, precision=lax.Precision.HIGHEST)
    pre = lax.psum(partial_pre, "ch")
    pooled = jax.nn.relu(norm_gain[4] * pre + norm_shift[4]).astype(jnp.bfloat16)
    blocks = w_proj.reshape(5, full, full)
    extended = extend_columns(features, kernel_reach)
    padded = jnp.pad(extended, ((kernel_reach, kernel_reach), (0, 0), (0, 0)))
    terms = branch_terms(padded, pointwise_weight, w_atrous, rows, cols, kernel_reach)
    sums = lax.psum_scatter(
        terms.astype(jnp.bfloat16), "ch", scatter_dimension=2, tiled=True
    ).astype(jnp.float32)
    gain = lax.dynamic_slice_in_dim(norm_gain, first, owned, 1)
    shift = lax.dynamic_slice_in_dim(norm_shift, first, owned, 1)
    branches = jax.nn.relu(sums * gain[:4] + shift[:4]).astype(jnp.bfloat16)
    pool_cols = lax.dynamic_slice_in_dim(blocks[4], first, owned, 1)
    pool_term = jnp.dot(pooled[None, :], pool_cols, preferred_element_type=jnp.float32)[0]
    own_cols = lax.dynamic_slice_in_dim(blocks[:4], first, owned, 2)
    projected = jnp.einsum(
        "pbk,bko->po",
        lax.all_gather(branches, "ch", axis=2, tiled=True),
        own_cols,
        preferred_element_type=jnp.float32,
    )
    head = jax.nn.relu(gain[5] * (projected + pool_term) + shift[5]).astype(jnp.bfloat16)
    return head.reshape(rows, cols, owned)


def solution(mesh):
    return jax.shard_map(
        local,
        mesh=mesh,
        in_specs=(
            P(None, "lon", "ch"),
            P("ch", None),
            P(None, None, None, "ch", None),
            P("ch", None),
            P(),
            P(),
            P(),
        ),
        out_specs=P(None, "lon", "ch"),
        check_vma=False,
    )
```

profile of v0, /device:TPU:1, one launch (start us, length us, event | category | flops | bytes accessed | tf_op | source)
XLA Modules:
  0.0 579.7 jit_solution(1187819210999614267)
XLA Ops:
  6.5 5.8 collective-permute-start.1
  12.3 2.3 collective-permute-start.2
  14.6 12.0 %collective-permute-start.3 = (bf16[80,15,128]{2,0,1:T(8,128)(2,1)}, bf16[80,15,128]{2,0,1:T(8,128)(2,1)S(1)}, u32[]{:S(2)}, u32[]{:S(2)}) collective-permute-start(bf16[80,15,128]{2,0,1:T(8,128)(2,1)} %param.7), channel_id=1, source_target_pairs={{0,496},{16,0},{32,16},{48,32},{64,48},{80,64},{96,80},{112,96},{1... | collective-permute-start | bytes 921608 | tf_op jit(solution)/shard_map/ppermute | solution.py:11
  26.7 4.3 collective-permute-start.4
  31.9 1.9 collective-permute-start
  33.9 2.7 fusion.57
  36.8 1.1 fusion.2
  37.9 7.8 %collective-permute-done = bf16[80,6,128]{2,0,1:T(8,128)(2,1)S(1)} collective-permute-done((bf16[80,6,128]{2,0,1:T(8,128)(2,1)S(1)}, bf16[80,6,128]{2,0,1:T(8,128)(2,1)S(1)}, u32[]{:S(2)}, u32[]{:S(2)}) %collective-permute-start) | collective-permute-done | bytes 122912 | tf_op jit(solution)/shard_map/ppermute | solution.py:11
  45.7 3.1 collective-permute-start.5
  49.1 3.4 collective-permute-done.5
  54.0 1.3 copy-done.3
  58.0 3.0 reshape.29
  61.0 2.3 copy.19
  63.3 3.0 reshape.28
  66.3 2.3 copy.18
  68.7 3.1 reshape.27
  71.7 3.0 fusion.5
  78.1 3.5 copy.21
  81.9 1.3 dynamic-slice.1
  83.9 289.4 %all-reduce.4.cloned.1.call-done = bf16[1200,4,256]{0,1,2:T(4,128)(2,1)} async-done(((bf16[1200,4,256]{0,1,2:T(4,128)(2,1)}), bf16[1200,4,256]{0,1,2:T(4,128)(2,1)}) %all-reduce.4.cloned.1.call-update) | async-done | bytes 2457616
  373.3 1.8 maximum_convert_fusion
  375.3 114.6 %psum.14 = f32[128]{0:T(128)S(1)} all-reduce(f32[128]{0:T(128)S(1)} %convert_reduce_fusion), channel_id=1, replica_groups=mesh['lon'=32,'ch'=16] {'lon'}, use_global_device_ids=true, to_apply=%region_2.0 | all-reduce | flops 128 | bytes 1024 | tf_op jit(solution)/shard_map/psum | solution.py:57
  490.1 79.1 %psum.15 = f32[256]{0:T(256)S(1)} all-reduce(f32[256]{0:T(256)S(1)} %bitcast.53), channel_id=1, replica_groups=mesh['lon'=32,'ch'=16] {'ch'}, use_global_device_ids=true, to_apply=%region_3.4 | all-reduce | flops 256 | bytes 2048 | tf_op jit(solution)/shard_map/psum | solution.py:59
  569.4 2.3 fusion.21
  (90 shorter events, 10.8 us)
Async XLA Ops:
  6.5 30.3 %copy-start = (bf16[128,256]{1,0:T(8,128)(2,1)S(1)}, bf16[128,256]{1,0:T(8,128)(2,1)}, u32[]{:S(2)}) copy-start(bf16[128,256]{1,0:T(8,128)(2,1)} %param.8) | copy-start | bytes 196612
  6.5 30.0 %copy-start.1 = (bf16[80,15,128]{2,0,1:T(8,128)(2,1)S(1)}, bf16[80,15,128]{2,0,1:T(8,128)(2,1)}, u32[]{:S(2)}) copy-start(bf16[80,15,128]{2,0,1:T(8,128)(2,1)} %param.7) | copy-start | bytes 921604
  6.5 366.7 %all-reduce.4.cloned.1.call-start = ((), (), s32[]{:S(2)}) async-start(), calls=%async_computation.1 | async-start | bytes 5242880
  6.5 42.3 %collective-permute-start.1 = (bf16[80,15,128]{2,0,1:T(8,128)(2,1)}, bf16[80,15,128]{2,0,1:T(8,128)(2,1)S(1)}, u32[]{:S(2)}, u32[]{:S(2)}) collective-permute-start(bf16[80,15,128]{2,0,1:T(8,128)(2,1)} %param.7), channel_id=1, source_target_pairs={{0,32},{16,48},{32,64},{48,80},{64,96},{80,112},{96,128},{112,144}... | collective-permute-start | bytes 921608 | tf_op jit(solution)/shard_map/ppermute | solution.py:11
  12.3 36.6 %collective-permute-start.2 = (bf16[80,15,128]{2,0,1:T(8,128)(2,1)}, bf16[80,15,128]{2,0,1:T(8,128)(2,1)S(1)}, u32[]{:S(2)}, u32[]{:S(2)}) collective-permute-start(bf16[80,15,128]{2,0,1:T(8,128)(2,1)} %param.7), channel_id=1, source_target_pairs={{0,16},{16,32},{32,48},{48,64},{64,80},{80,96},{96,112},{112,128},... | collective-permute-start | bytes 921608 | tf_op jit(solution)/shard_map/ppermute | solution.py:11
  14.6 34.4 %collective-permute-start.3 = (bf16[80,15,128]{2,0,1:T(8,128)(2,1)}, bf16[80,15,128]{2,0,1:T(8,128)(2,1)S(1)}, u32[]{:S(2)}, u32[]{:S(2)}) collective-permute-start(bf16[80,15,128]{2,0,1:T(8,128)(2,1)} %param.7), channel_id=1, source_target_pairs={{0,496},{16,0},{32,16},{48,32},{64,48},{80,64},{96,80},{112,96},{1... | collective-permute-start | bytes 921608 | tf_op jit(solution)/shard_map/ppermute | solution.py:11
  26.7 22.4 %collective-permute-start.4 = (bf16[80,15,128]{2,0,1:T(8,128)(2,1)}, bf16[80,15,128]{2,0,1:T(8,128)(2,1)S(1)}, u32[]{:S(2)}, u32[]{:S(2)}) collective-permute-start(bf16[80,15,128]{2,0,1:T(8,128)(2,1)} %param.7), channel_id=1, source_target_pairs={{0,480},{16,496},{32,0},{48,16},{64,32},{80,48},{96,64},{112,80},{... | collective-permute-start | bytes 921608 | tf_op jit(solution)/shard_map/ppermute | solution.py:11
  31.9 13.8 %collective-permute-start = (bf16[80,6,128]{2,0,1:T(8,128)(2,1)S(1)}, bf16[80,6,128]{2,0,1:T(8,128)(2,1)S(1)}, u32[]{:S(2)}, u32[]{:S(2)}) collective-permute-start(bf16[80,6,128]{2,0,1:T(8,128)(2,1)S(1)} %get-tuple-element.14), channel_id=1, source_target_pairs={{0,48},{16,64},{32,80},{48,96},{64,112},{80,128},{96,144},{112,160... | collective-permute-start | bytes 368648 | tf_op jit(solution)/shard_map/ppermute | solution.py:11
  45.7 6.8 %collective-permute-start.5 = (bf16[80,6,128]{2,0,1:T(8,128)(2,1)S(1)}, bf16[80,6,128]{2,0,1:T(8,128)(2,1)S(1)}, u32[]{:S(2)}, u32[]{:S(2)}) collective-permute-start(bf16[80,6,128]{2,0,1:T(8,128)(2,1)S(1)} %get-tuple-element.13), channel_id=1, source_target_pairs={{0,464},{16,480},{32,496},{48,0},{64,16},{80,32},{96,48},{112,64},... | collective-permute-start | bytes 368648 | tf_op jit(solution)/shard_map/ppermute | solution.py:11
  53.6 1.6 copy-start.3
  55.7 1.5 copy-start.2
  71.7 3.0 copy-start.4
  71.7 3.0 copy-start.8
  74.8 1.8 copy-start.5
  74.8 1.9 copy-start.7
  76.7 1.1 copy-start.6
  78.0 3.6 copy-start.10
  78.1 3.6 copy-start.11
  81.6 408.4 %copy-start.9 = (bf16[128,256]{1,0:T(8,128)(2,1)S(1)}, bf16[128,256]{1,0:T(8,128)(2,1)}, u32[]{:S(2)}) copy-start(bf16[128,256]{1,0:T(8,128)(2,1)} %param.10) | copy-start | bytes 196612
  81.6 487.6 %slice-start = ((bf16[1280,256]{1,0:T(8,128)(2,1)}), bf16[256,256]{1,0:T(8,128)(2,1)S(1)}, s32[]{:S(2)}) async-start(bf16[1280,256]{1,0:T(8,128)(2,1)} %param.11), calls=%async_computation.2 | async-start | bytes 262144 | tf_op jit(solution)/shard_map/slice | solution.py:71
  81.6 487.8 %slice-start.1 = ((bf16[1280,256]{1,0:T(8,128)(2,1)}), bf16[1024,256]{1,0:T(8,128)(2,1)S(1)}, s32[]{:S(2)}) async-start(bf16[1280,256]{1,0:T(8,128)(2,1)} %param.11), calls=%async_computation.3 | async-start | bytes 1048576 | tf_op jit(solution)/shard_map/slice | solution.py:73
  81.6 487.8 %all-gather.2.cloned.1.call-start = ((), (), s32[]{:S(2)}) async-start(), calls=%async_computation | async-start | bytes 2785280 | tf_op jit(solution)/shard_map/all_gather | solution.py:76
Sparse Core Ops, SparseCore 0:
  81.7 291.5 all-reduce.3
  376.6 100.9 all-gather.1
where the time goes:
time: 580 us
  waiting for transfers between devices  301 us (52%)
  blocking collectives  194 us (33%)
  local copies, waits for them, and re-layouts  29.9 us (5%)
  starting transfers between devices  29.4 us (5%)
  between operations  14.5 us (2%)
  matrix products  8.72 us (2%)
    unnamed x3, waiting for transfers between devices  289 us
    psum x1, blocking collectives, local(): column_total = lax.psum(local_sum, 'lon')  115 us
    psum x1, blocking collectives, local(): pre = lax.psum(partial_pre, 'ch')  79.1 us
    ppermute x6, starting transfers between devices, from_behind(): lax.ppermute(value, axis, [(i, (i + by) % count) for i in range(count)])  29.4 us
  transfers between devices with their start and end apart: 8, of which 3 were waited for; matrix products, arithmetic and copies ran while one was open for 1% of the time, Pallas kernels for 0%

commit v1 on v0

v1 whole, which is shorter than its diff:
```python
import jax
import jax.numpy as jnp
from jax import lax
from jax.experimental import pallas as pl
from jax.experimental.pallas import tpu as pltpu
from jax.sharding import PartitionSpec as P

MESH_ID = pl.DeviceIdType.MESH
F32 = jnp.float32
BF16 = jnp.bfloat16

PAD = 48


def head_kernel(
    feat, pw, wa, wpool, wproj, gain, shift, out,
    xin, xb, part, cbuf, xbuf, zsrc, zown, zbuf, stage, obuf,
    pwv, wav, wprojv, poolsrc, poolbuf,
    ld_sem, ys, yr, hs, hr, cs, cr, xs, xr, zs, zr, os, orr, ps, pr,
):
    lon = lax.axis_index("lon")
    ch = lax.axis_index("ch")
    zl, y = lon // 4, lon % 4
    zh, x, c = ch // 8, (ch // 2) % 4, ch % 2

    def at(zl_=None, y_=None, zh_=None, x_=None, c_=None):
        zz = zl if zl_ is None else zl_
        yy = y if y_ is None else y_
        hh = zh if zh_ is None else zh_
        xx = x if x_ is None else x_
        cc = c if c_ is None else c_
        return (zz * 4 + yy, hh * 8 + xx * 2 + cc)

    k = c * 8 + x * 2 + zh
    kq, kt = k // 3, k % 3
    kg = 4 * kq + y
    y_dst = kg // 5
    slot = (kg % 5) * 3 + kt
    has_col = k < 15

    loads = [
        pltpu.make_async_copy(feat, xin, ld_sem.at[0]),
        pltpu.make_async_copy(pw, pwv, ld_sem.at[1]),
        pltpu.make_async_copy(wa, wav, ld_sem.at[2]),
        pltpu.make_async_copy(wproj, wprojv, ld_sem.at[3]),
    ]
    for load in loads:
        load.start()

    barrier = pltpu.get_barrier_semaphore()

    def hello(dev):
        pl.semaphore_signal(barrier, inc=1, device_id=dev, device_id_type=MESH_ID)

    for d in range(1, 8):
        hello(at(zl_=(zl + d) % 8))
    hello(at(zh_=1 - zh))
    hello(at(c_=1 - c))
    for d in range(1, 4):
        hello(at(y_=(y + d) % 4))
        hello(at(x_=(x + d) % 4))

    def source(i):
        g = 5 * y + i // 3
        kk = (g // 4) * 3 + i % 3
        return (g % 4), (kk % 2) * 8 + ((kk // 2) % 4) * 2 + kk // 8

    def greet(i, carry):
        sy, sch = source(i)

        @pl.when(jnp.logical_or(sy != y, sch != ch))
        def _():
            hello((zl * 4 + sy, sch))

        return carry

    lax.fori_loop(0, 15, greet, 0)

    zrow = jnp.zeros((3, PAD, 128), BF16)

    def clear(i, carry):
        xb[i, :, pl.ds(0, PAD), :] = zrow
        xb[i, :, pl.ds(PAD + 80, PAD), :] = zrow
        return carry

    lax.fori_loop(0, 11, clear, 0)
    for b in range(4):
        part[b, 15] = jnp.zeros((80, 256), BF16)

    loads[0].wait()
    xb[y + 3, :, pl.ds(PAD, 80), :] = xin[0:3]
    xb[y + 4, :, pl.ds(PAD, 80), :] = xin[12:15]

    def add_col(i, acc):
        return acc + jnp.sum(xin[i].astype(F32).reshape(10, 8, 128), axis=0)

    acc = lax.fori_loop(0, 15, add_col, jnp.zeros((8, 128), F32))
    colsum = jnp.sum(acc, axis=0, keepdims=True)
    pre = jnp.dot(
        jnp.broadcast_to(colsum, (8, 128)), wpool[...].astype(F32),
        precision=lax.Precision.HIGHEST, preferred_element_type=F32,
    )[0:1]
    poolsrc[0] = pre

    own_signals = jnp.where(y_dst == y, 15, 16) * has_col.astype(jnp.int32)
    pl.semaphore_wait(barrier, 15 + own_signals)

    def remote(src, dst, ssem, rsem, dev):
        return pltpu.make_async_remote_copy(
            src_ref=src, dst_ref=dst, send_sem=ssem, recv_sem=rsem,
            device_id=dev, device_id_type=MESH_ID,
        )

    rows = pl.ds(PAD, 80)
    ycopies = []
    for g in range(1, 4):
        q = (5 * y + g) // 4
        copy = remote(
            xin.at[pl.ds(3 * g, 3)], xb.at[q + 3, :, rows, :],
            ys.at[g - 1], yr.at[g - 1], at(y_=(y + g) % 4),
        )
        copy.start()
        ycopies.append(copy)
    psends = []

    def pool_send(stage_i, slot_i, dev):
        copy = remote(poolsrc.at[stage_i], poolbuf.at[slot_i], ps.at[slot_i], pr.at[slot_i], dev)
        copy.start()
        psends.append(copy)

    def pool_sum(stage_i, slots):
        tot = poolsrc[stage_i]
        for s in slots:
            psends[s].wait_recv()
            tot = tot + poolbuf[s]
        return tot

    for d in range(1, 4):
        pool_send(0, d - 1, at(y_=(y + d) % 4))
    for copy in ycopies:
        copy.wait_recv()

    halo = []
    for d in range(3):
        for side in range(2):
            q = (4 - d) if side == 0 else d
            q_to = q - 5 if side == 0 else q + 5
            dev = at(zl_=(zl + 1) % 8) if side == 0 else at(zl_=(zl + 7) % 8)
            copy = remote(
                xb.at[q + 3, :, rows, :], xb.at[q_to + 3, :, rows, :],
                hs.at[2 * d + side], hr.at[2 * d + side], dev,
            )
            copy.start()
            halo.append(copy)

    loads[1].wait()
    loads[2].wait()

    def compute(b):
        def body(q, carry):
            if b == 0:
                lhs = xb[q + 3, :, rows, :].reshape(240, 128)
                res = jnp.dot(lhs, pwv[...], preferred_element_type=F32)
            else:
                taps = []
                for ro in (-1, 0, 1):
                    for co in (-1, 0, 1):
                        taps.append(
                            xb[q + 3 + co * b, :, pl.ds(PAD + ro * b * 12, 80), :].reshape(240, 128)
                        )
                res = jnp.dot(
                    jnp.concatenate(taps, axis=1), wav[b - 1].reshape(1152, 256),
                    preferred_element_type=F32,
                )
            part[b, pl.ds(3 * q, 3)] = res.astype(BF16).reshape(3, 80, 256)
            return carry

        lax.fori_loop(0, 5, body, 0)

    core_copies, x_copies, z_copies = {}, {}, {}

    def core_send(b):
        copy = remote(
            part.at[b, pl.ds((1 - c) * 8, 8)], cbuf.at[b], cs.at[b], cr.at[b], at(c_=1 - c)
        )
        copy.start()
        core_copies[b] = copy

    def core_reduce(b):
        core_copies[b].wait_recv()

        def body(i, carry):
            mine = part[b, c * 8 + i].astype(F32) + cbuf[b, i].astype(F32)
            part[b, c * 8 + i] = mine.astype(BF16)
            return carry

        lax.fori_loop(0, 8, body, 0)
        x_copies[b] = []
        for d in range(1, 4):
            to = (x + d) % 4
            copy = remote(
                part.at[b, pl.ds(c * 8 + to * 2, 2)], xbuf.at[b, d - 1],
                xs.at[b, d - 1], xr.at[b, d - 1], at(x_=to),
            )
            copy.start()
            x_copies[b].append(copy)

    def x_reduce(b):
        for copy in x_copies[b]:
            copy.wait_recv()

        def total(j):
            t = part[b, c * 8 + x * 2 + j].astype(F32)
            for d in range(3):
                t = t + xbuf[b, d, j].astype(F32)
            return t

        zsrc[b] = total(1 - zh).astype(BF16)
        copy = remote(zsrc.at[b], zbuf.at[b], zs.at[b], zr.at[b], at(zh_=1 - zh))
        copy.start()
        z_copies[b] = copy
        zown[b] = total(zh)

    def halo_wait(d):
        halo[2 * d].wait_recv()
        halo[2 * d + 1].wait_recv()

    compute(0)
    core_send(0)
    poolsrc[1] = pool_sum(0, range(0, 3))
    for d in range(1, 8):
        pool_send(1, 2 + d, at(zl_=(zl + d) % 8))
    halo_wait(0)
    compute(1)
    core_send(1)
    core_reduce(0)
    halo_wait(1)
    compute(2)
    core_send(2)
    core_reduce(1)
    x_reduce(0)
    poolsrc[2] = pool_sum(1, range(3, 10))
    pool_send(2, 10, at(c_=1 - c))
    halo_wait(2)
    compute(3)
    core_send(3)
    core_reduce(2)
    poolsrc[3] = pool_sum(2, (10,))
    for d in range(1, 4):
        pool_send(3, 10 + d, at(x_=(x + d) % 4))
    x_reduce(1)
    core_reduce(3)
    poolsrc[4] = pool_sum(3, range(11, 14))
    pool_send(4, 14, at(zh_=1 - zh))
    x_reduce(2)
    x_reduce(3)
    loads[3].wait()

    proj = jnp.zeros((80, 256), F32)
    for b in range(4):
        z_copies[b].wait_recv()
        total = zown[b] + zbuf[b].astype(F32)
        act = jnp.maximum(total * gain[b : b + 1] + shift[b : b + 1], 0.0).astype(BF16)
        proj = proj + jnp.dot(act, wprojv[pl.ds(b * 256, 256), :], preferred_element_type=F32)
    pre_all = pool_sum(4, (14,)) * (1.0 / 38400.0)
    pooled = jnp.maximum(gain[4:5] * pre_all + shift[4:5], 0.0).astype(BF16)
    pool_term = jnp.dot(
        jnp.broadcast_to(pooled, (16, 256)), wprojv[pl.ds(1024, 256), :], preferred_element_type=F32
    )[0:1]
    head = jnp.maximum(gain[5:6] * (proj + pool_term) + shift[5:6], 0.0)
    head = jnp.concatenate([head, jnp.zeros((48, 256), F32)], axis=0)
    stage[...] = jnp.transpose(head).astype(BF16).reshape(16, 16, 128)

    def out_copy(d):
        return remote(stage.at[d], obuf.at[slot], os.at[d], orr.at[slot], (zl * 4 + y_dst, d))

    def is_self(d):
        return jnp.logical_and(y_dst == y, d == ch)

    def out_send(i, carry):
        d = (ch + i) % 16

        @pl.when(jnp.logical_and(has_col, jnp.logical_not(is_self(d))))
        def _():
            out_copy(d).start()

        return carry

    lax.fori_loop(0, 16, out_send, 0)

    @pl.when(jnp.logical_and(has_col, y_dst == y))
    def _():
        pltpu.make_async_copy(stage.at[ch], obuf.at[slot], orr.at[slot]).start()

    def out_recv(i, carry):
        pltpu.make_async_copy(stage.at[0], obuf.at[i], orr.at[i]).wait()
        return carry

    lax.fori_loop(0, 15, out_recv, 0)
    out[...] = obuf[:, :, 0:80]

    def out_sent(d, carry):
        @pl.when(jnp.logical_and(has_col, jnp.logical_not(is_self(d))))
        def _():
            out_copy(d).wait_send()

        return carry

    lax.fori_loop(0, 16, out_sent, 0)
    for copy in ycopies + halo + psends:
        copy.wait_send()
    for b in range(4):
        core_copies[b].wait_send()
        for copy in x_copies[b]:
            copy.wait_send()
        z_copies[b].wait_send()


def local(features, pointwise_weight, w_atrous, w_pool, w_proj, norm_gain, norm_shift):
    feat = jnp.transpose(features, (1, 0, 2))
    vmem = pl.BlockSpec(memory_space=pltpu.VMEM)
    hbm = pl.BlockSpec(memory_space=pl.ANY)
    dma = pltpu.SemaphoreType.DMA
    out = pl.pallas_call(
        head_kernel,
        out_shape=jax.ShapeDtypeStruct((15, 16, 80), BF16),
        in_specs=[hbm, hbm, hbm, vmem, hbm, vmem, vmem],
        out_specs=vmem,
        scratch_shapes=[
            pltpu.VMEM((15, 80, 128), BF16),
            pltpu.VMEM((11, 3, 80 + 2 * PAD, 128), BF16),
            pltpu.VMEM((4, 16, 80, 256), BF16),
            pltpu.VMEM((4, 8, 80, 256), BF16),
            pltpu.VMEM((4, 3, 2, 80, 256), BF16),
            pltpu.VMEM((4, 80, 256), BF16),
            pltpu.VMEM((4, 80, 256), F32),
            pltpu.VMEM((4, 80, 256), BF16),
            pltpu.VMEM((16, 16, 128), BF16),
            pltpu.VMEM((15, 16, 128), BF16),
            pltpu.VMEM((128, 256), BF16),
            pltpu.VMEM((3, 9, 128, 256), BF16),
            pltpu.VMEM((1280, 256), BF16),
            pltpu.VMEM((5, 1, 256), F32),
            pltpu.VMEM((15, 1, 256), F32),
            dma((4,)),
            dma((3,)), dma((3,)),
            dma((6,)), dma((6,)),
            dma((4,)), dma((4,)),
            dma((4, 3)), dma((4, 3)),
            dma((4,)), dma((4,)),
            dma((16,)), dma((15,)),
            dma((15,)), dma((15,)),
        ],
        compiler_params=pltpu.CompilerParams(collective_id=0, has_side_effects=True),
        name="aspp_head",
    )(
        feat, pointwise_weight, w_atrous.reshape(3, 9, 128, 256), w_pool, w_proj,
        norm_gain, norm_shift,
    )
    return jnp.transpose(out, (2, 0, 1))


def solution(mesh):
    return jax.shard_map(
        local,
        mesh=mesh,
        in_specs=(
            P(None, "lon", "ch"),
            P("ch", None),
            P(None, None, None, "ch", None),
            P("ch", None),
            P(),
            P(),
            P(),
        ),
        out_specs=P(None, "lon", "ch"),
        check_vma=False,
    )
```

time: 580 us -> 72.3 us (0.12)
  waiting for transfers between devices: 301 us -> 0 us
  blocking collectives: 194 us -> 0 us
  Pallas kernels: 0 us -> 70.6 us
  starting transfers between devices: 29.4 us -> 0 us
  local copies, waits for them, and re-layouts: 29.9 us -> 1.46 us
  between operations: 14.5 us -> 0.01 us
  matrix products: 8.72 us -> 0 us
    unnamed x3 -> x0, waiting for transfers between devices: 289 us -> none
    psum x2 -> x0, blocking collectives: 194 us -> none  [the longest x1 115 us: local(): column_total = lax.psum(local_sum, 'lon')]
    pallas_call x0 -> x1, Pallas kernels: none -> 70.6 us  [local(): pl.pallas_call(head_kernel, out_shape=jax.ShapeDtypeStruct((15, 16, 80),...]
    ppermute x6 -> x0, starting transfers between devices: 29.4 us -> none  [from_behind(): lax.ppermute(value, axis, [(i, (i + by) % count) for i in range(count)])]
    ppermute x6 -> x0, waiting for transfers between devices: 11.3 us -> none  [from_behind(): lax.ppermute(value, axis, [(i, (i + by) % count) for i in range(count)])]
    reshape x6 -> x0, local copies, waits for them, and re-layouts: 10.3 us -> none  [the longest x3 9.02 us: branch_terms(): stacked = jnp.concatenate(taps, axis=2).reshape(pixels, 9 * chans)]
    dot_general x7 -> x0, matrix products: 8.72 us -> none  [the longest x3 4.95 us: branch_terms(): terms.append(jnp.dot(stacked, kernel, preferred_element_type=jnp.float32))]
  transfers between devices with their start and end apart: 8 -> 0, of which waited for: 3 -> 0; matrix products, arithmetic and copies ran while one was open for 1% -> 0% of each run, Pallas kernels for 0% -> 0%
where the time goes in v1:
time: 72.3 us; the launch traced here: 72.1 us
  Pallas kernels  70.6 us (98%)
  local copies, waits for them, and re-layouts  1.46 us (2%)
    pallas_call x1, Pallas kernels, local(): pl.pallas_call(head_kernel, out_shape=jax.ShapeDtypeStruct((15, 16, 80),...  70.6 us
    unnamed x1, local copies, waits for them, and re-layouts  1.46 us

profile of v1, /device:TPU:1, one launch (start us, length us, event | category | flops | bytes accessed | tf_op | source)
XLA Modules:
  0.0 72.1 jit_solution(15802348121525225089)
XLA Ops:
  0.0 70.6 %aspp_head.1 = bf16[15,16,80]{2,1,0:T(8,128)(2,1)} custom-call(bf16[15,80,128]{2,1,0:T(8,128)(2,1)} %bitcast.4, bf16[128,256]{1,0:T(8,128)(2,1)} %pw.1, bf16[3,9,128,256]{3,2,1,0:T(8,128)(2,1)} %bitcast.3, bf16[128,256]{1,0:T(8,128)(2,1)} %wpool.1, bf16[1280,256]{1,0:T(8,128)(2,1)} %wproj.1, f32[6,256]{1,0:T(8,128)} %gain.1, f32[6,256]{1,0:T(8,128)} %shift.1), custom_call_target="tpu_custom_call" | custom-call | tf_op jit(solution)/shard_map/aspp_head/pallas_call | solution.py:324
  70.6 1.5 %copy.9 = bf16[80,15,16]{0,2,1:T(8,128)(2,1)} copy(bf16[80,15,16]{0,2,1:T(8,128)(2,1)} %bitcast.5) | data formatting | bytes 76800

commit v2 on v1

v2 whole, which is shorter than its diff:
```python
import jax
import jax.numpy as jnp
from jax import lax
from jax.experimental import pallas as pl
from jax.experimental.pallas import tpu as pltpu
from jax.sharding import PartitionSpec as P

MESH_ID = pl.DeviceIdType.MESH
F32 = jnp.float32
BF16 = jnp.bfloat16

PAD = 48


def head_kernel(
    feat, pw, wa, wpool, wproj, gain, shift, out,
    xin, xb, part, cbuf, xbuf, zsrc, zbuf, stage, obuf,
    pwv, wav, wprojv, poolsrc, poolbuf,
    ld_sem, ys, yr, hs, hr, cs, cr, xs, xr, zs, zr, os, orr, ps, pr,
):
    lon = lax.axis_index("lon")
    ch = lax.axis_index("ch")
    zl, y = lon // 4, lon % 4
    zh, x, c = ch // 8, (ch // 2) % 4, ch % 2
    z = zh * 8 + zl

    def at(zl_=None, y_=None, x_=None, c_=None):
        zz = zl if zl_ is None else zl_
        yy = y if y_ is None else y_
        xx = x if x_ is None else x_
        cc = c if c_ is None else c_
        return (zz * 4 + yy, zh * 8 + xx * 2 + cc)

    def at_z(dz):
        zz = (z + dz) % 16
        return ((zz % 8) * 4 + y, (zz // 8) * 8 + x * 2 + c)

    bit = ((z + 12) % 16) // 8
    k = c * 8 + x * 2 + bit
    kq, kt = k // 3, k % 3
    kg = 4 * kq + y
    y_dst = kg // 5
    slot = (kg % 5) * 3 + kt
    has_col = k < 15
    zl_dst = (zl + 4) % 8

    loads = [
        pltpu.make_async_copy(feat, xin, ld_sem.at[0]),
        pltpu.make_async_copy(pw, pwv, ld_sem.at[1]),
        pltpu.make_async_copy(wa, wav, ld_sem.at[2]),
        pltpu.make_async_copy(wproj, wprojv, ld_sem.at[3]),
    ]
    for load in loads:
        load.start()

    barrier = pltpu.get_barrier_semaphore()

    def hello(dev):
        pl.semaphore_signal(barrier, inc=1, device_id=dev, device_id_type=MESH_ID)

    east, west = at(zl_=(zl + 1) % 8), at(zl_=(zl + 7) % 8)
    hello(east)
    hello(west)
    hello(at_z(4))
    hello(at_z(12))

    def greet(i, carry):
        g = 5 * y + i // 3
        kk = (g // 4) * 3 + i % 3
        zz = (zl + 4 + 8 * (kk % 2)) % 16
        hello(((zz % 8) * 4 + g % 4, (zz // 8) * 8 + ((kk // 2) % 4) * 2 + kk // 8))
        return carry

    lax.fori_loop(0, 15, greet, 0)
    for d in range(1, 4):
        hello(at(y_=(y + d) % 4))
        hello(at(x_=(x + d) % 4))
    hello(at(c_=1 - c))

    zrow = jnp.zeros((3, PAD, 128), BF16)

    def clear(i, carry):
        xb[i, :, pl.ds(0, PAD), :] = zrow
        xb[i, :, pl.ds(PAD + 80, PAD), :] = zrow
        return carry

    lax.fori_loop(0, 11, clear, 0)
    for b in range(4):
        part[b, 15] = jnp.zeros((80, 256), BF16)

    loads[0].wait()

    def add_col(i, acc):
        return acc + jnp.sum(xin[i].astype(F32).reshape(10, 8, 128), axis=0)

    acc = lax.fori_loop(0, 15, add_col, jnp.zeros((8, 128), F32))
    colsum = jnp.sum(acc, axis=0, keepdims=True)
    pre = jnp.dot(
        jnp.broadcast_to(colsum, (8, 128)), wpool[...].astype(F32),
        precision=lax.Precision.HIGHEST, preferred_element_type=F32,
    )[0:1]
    poolsrc[0] = pre

    pl.semaphore_wait(barrier, 11 + 16 * has_col.astype(jnp.int32))

    def remote(src, dst, ssem, rsem, dev):
        return pltpu.make_async_remote_copy(
            src_ref=src, dst_ref=dst, send_sem=ssem, recv_sem=rsem,
            device_id=dev, device_id_type=MESH_ID,
        )

    rows = pl.ds(PAD, 80)
    ycopies = []
    for g in range(1, 4):
        q = (5 * y + g) // 4
        copy = remote(
            xin.at[pl.ds(3 * g, 3)], xb.at[q + 3, :, rows, :],
            ys.at[g - 1], yr.at[g - 1], at(y_=(y + g) % 4),
        )
        copy.start()
        ycopies.append(copy)
    psends = []

    def pool_send(src, slot_i, dev):
        copy = remote(src, poolbuf.at[slot_i], ps.at[slot_i], pr.at[slot_i], dev)
        copy.start()
        psends.append(copy)

    def pool_get(slot_i):
        psends[slot_i].wait_recv()
        return poolbuf[slot_i]

    for d in range(1, 4):
        pool_send(poolsrc.at[0], d - 1, at(y_=(y + d) % 4))
    xb[y + 3, :, rows, :] = xin[0:3]
    xb[y + 4, :, rows, :] = xin[12:15]
    for copy in ycopies:
        copy.wait_recv()

    halo = []
    for d in range(3):
        for side in range(2):
            q = (4 - d) if side == 0 else d
            q_to = q - 5 if side == 0 else q + 5
            copy = remote(
                xb.at[q + 3, :, rows, :], xb.at[q_to + 3, :, rows, :],
                hs.at[2 * d + side], hr.at[2 * d + side], east if side == 0 else west,
            )
            copy.start()
            halo.append(copy)

    late = jnp.where(zl == 0, 0, 1)

    def halo_wait(d, side):
        remote(
            xb.at[3, :, rows, :], xb.at[4, :, rows, :],
            hs.at[2 * d + side], hr.at[2 * d + side], east,
        ).wait_recv()

    loads[1].wait()
    loads[2].wait()

    def compute(b, lo, hi):
        def body(j, carry):
            q = jnp.where(late == 1, j, 4 - j)
            if b == 0:
                lhs = xb[q + 3, :, rows, :].reshape(240, 128)
                res = jnp.dot(lhs, pwv[...], preferred_element_type=F32)
            else:
                taps = []
                for ro in (-1, 0, 1):
                    for co in (-1, 0, 1):
                        taps.append(
                            xb[q + 3 + co * b, :, pl.ds(PAD + ro * b * 12, 80), :].reshape(240, 128)
                        )
                res = jnp.dot(
                    jnp.concatenate(taps, axis=1), wav[b - 1].reshape(1152, 256),
                    preferred_element_type=F32,
                )
            part[b, pl.ds(3 * q, 3)] = res.astype(BF16).reshape(3, 80, 256)
            return carry

        lax.fori_loop(lo, hi, body, 0)

    core_copies, x_copies, z_copies = {}, {}, {}

    def core_send(b):
        copy = remote(
            part.at[b, pl.ds((1 - c) * 8, 8)], cbuf.at[b], cs.at[b], cr.at[b], at(c_=1 - c)
        )
        copy.start()
        core_copies[b] = copy

    def core_reduce(b):
        core_copies[b].wait_recv()

        def body(i, carry):
            mine = part[b, c * 8 + i].astype(F32) + cbuf[b, i].astype(F32)
            part[b, c * 8 + i] = mine.astype(BF16)
            return carry

        lax.fori_loop(0, 8, body, 0)
        x_copies[b] = []
        for d in range(1, 4):
            to = (x + d) % 4
            copy = remote(
                part.at[b, pl.ds(c * 8 + to * 2, 2)], xbuf.at[b, d - 1],
                xs.at[b, d - 1], xr.at[b, d - 1], at(x_=to),
            )
            copy.start()
            x_copies[b].append(copy)

    def x_reduce(b):
        for copy in x_copies[b]:
            copy.wait_recv()
        for j in range(2):
            t = part[b, c * 8 + x * 2 + j].astype(F32)
            for d in range(3):
                t = t + xbuf[b, d, j].astype(F32)
            zsrc[b, j] = t.astype(BF16)
        z_copies[b] = []
        for way in range(2):
            j = zh if way == 0 else 1 - zh
            copy = remote(
                zsrc.at[b, j], zbuf.at[b, way], zs.at[b, way], zr.at[b, way],
                at_z(4) if way == 0 else at_z(12),
            )
            copy.start()
            z_copies[b].append(copy)

    compute(0, 0, 5)
    core_send(0)
    own = poolsrc[0] + pool_get(0) + pool_get(1) + pool_get(2)
    poolsrc[1] = own
    pool_send(poolsrc.at[1], 3, east)
    pool_send(poolsrc.at[1], 4, west)
    core_reduce(0)
    for b in range(1, 4):
        halo_wait(b - 1, 1 - late)
        compute(b, 0, 5 - b)
    halo_wait(0, late)
    compute(1, 4, 5)
    core_send(1)
    x_reduce(0)
    three = own + pool_get(3) + pool_get(4)
    pool_send(poolbuf.at[4], 5, west)
    core_reduce(1)
    halo_wait(1, late)
    compute(2, 3, 5)
    core_send(2)
    x_reduce(1)
    core_reduce(2)
    halo_wait(2, late)
    compute(3, 2, 5)
    core_send(3)
    four = three + pool_get(5)
    poolsrc[2] = four
    pool_send(poolsrc.at[2], 6, at_z(4))
    pool_send(poolsrc.at[2], 7, at_z(12))
    x_reduce(2)
    core_reduce(3)
    twelve = four + pool_get(6) + pool_get(7)
    pool_send(poolbuf.at[7], 8, at_z(12))
    x_reduce(3)
    all_z = twelve + pool_get(8)
    poolsrc[3] = all_z
    pool_send(poolsrc.at[3], 9, at(c_=1 - c))
    loads[3].wait()

    proj = jnp.zeros((80, 256), F32)
    for b in range(4):
        if b == 2:
            both = all_z + pool_get(9)
            poolsrc[4] = both
            for d in range(1, 4):
                pool_send(poolsrc.at[4], 9 + d, at(x_=(x + d) % 4))
        if b == 3:
            pre_all = both + pool_get(10) + pool_get(11) + pool_get(12)
            pre_all = pre_all * (1.0 / 38400.0)
            pooled = jnp.maximum(gain[4:5] * pre_all + shift[4:5], 0.0).astype(BF16)
            pool_term = jnp.dot(
                jnp.broadcast_to(pooled, (16, 256)), wprojv[pl.ds(1024, 256), :],
                preferred_element_type=F32,
            )[0:1]
        for copy in z_copies[b]:
            copy.wait_recv()
        total = zbuf[b, 0].astype(F32) + zbuf[b, 1].astype(F32)
        act = jnp.maximum(total * gain[b : b + 1] + shift[b : b + 1], 0.0).astype(BF16)
        proj = proj + jnp.dot(act, wprojv[pl.ds(b * 256, 256), :], preferred_element_type=F32)
    head = jnp.maximum(gain[5:6] * (proj + pool_term) + shift[5:6], 0.0)
    head = jnp.concatenate([head, jnp.zeros((48, 256), F32)], axis=0)
    stage[...] = jnp.transpose(head).astype(BF16).reshape(16, 16, 128)

    def out_copy(d):
        return remote(stage.at[d], obuf.at[slot], os.at[d], orr.at[slot], (zl_dst * 4 + y_dst, d))

    def out_send(i, carry):
        @pl.when(has_col)
        def _():
            out_copy((ch + i) % 16).start()

        return carry

    lax.fori_loop(0, 16, out_send, 0)
    for copy in ycopies + halo + psends:
        copy.wait_send()
    for b in range(4):
        core_copies[b].wait_send()
        for copy in x_copies[b] + z_copies[b]:
            copy.wait_send()

    def out_recv(i, carry):
        remote(stage.at[0], obuf.at[i], os.at[0], orr.at[i], east).wait_recv()
        return carry

    lax.fori_loop(0, 15, out_recv, 0)
    out[...] = obuf[:, :, 0:80]

    def out_sent(d, carry):
        @pl.when(has_col)
        def _():
            out_copy(d).wait_send()

        return carry

    lax.fori_loop(0, 16, out_sent, 0)


def local(features, pointwise_weight, w_atrous, w_pool, w_proj, norm_gain, norm_shift):
    feat = jnp.transpose(features, (1, 0, 2))
    vmem = pl.BlockSpec(memory_space=pltpu.VMEM)
    hbm = pl.BlockSpec(memory_space=pl.ANY)
    dma = pltpu.SemaphoreType.DMA
    out = pl.pallas_call(
        head_kernel,
        out_shape=jax.ShapeDtypeStruct((15, 16, 80), BF16),
        in_specs=[hbm, hbm, hbm, vmem, hbm, vmem, vmem],
        out_specs=vmem,
        scratch_shapes=[
            pltpu.VMEM((15, 80, 128), BF16),
            pltpu.VMEM((11, 3, 80 + 2 * PAD, 128), BF16),
            pltpu.VMEM((4, 16, 80, 256), BF16),
            pltpu.VMEM((4, 8, 80, 256), BF16),
            pltpu.VMEM((4, 3, 2, 80, 256), BF16),
            pltpu.VMEM((4, 2, 80, 256), BF16),
            pltpu.VMEM((4, 2, 80, 256), BF16),
            pltpu.VMEM((16, 16, 128), BF16),
            pltpu.VMEM((15, 16, 128), BF16),
            pltpu.VMEM((128, 256), BF16),
            pltpu.VMEM((3, 9, 128, 256), BF16),
            pltpu.VMEM((1280, 256), BF16),
            pltpu.VMEM((5, 1, 256), F32),
            pltpu.VMEM((13, 1, 256), F32),
            dma((4,)),
            dma((3,)), dma((3,)),
            dma((6,)), dma((6,)),
            dma((4,)), dma((4,)),
            dma((4, 3)), dma((4, 3)),
            dma((4, 2)), dma((4, 2)),
            dma((16,)), dma((15,)),
            dma((13,)), dma((13,)),
        ],
        compiler_params=pltpu.CompilerParams(collective_id=0, has_side_effects=True),
        name="aspp_head",
    )(
        feat, pointwise_weight, w_atrous.reshape(3, 9, 128, 256), w_pool, w_proj,
        norm_gain, norm_shift,
    )
    return jnp.transpose(out, (2, 0, 1))


def solution(mesh):
    return jax.shard_map(
        local,
        mesh=mesh,
        in_specs=(
            P(None, "lon", "ch"),
            P("ch", None),
            P(None, None, None, "ch", None),
            P("ch", None),
            P(),
            P(),
            P(),
        ),
        out_specs=P(None, "lon", "ch"),
        check_vma=False,
    )
```

time: 72.3 us -> 69.2 us (0.957)
  Pallas kernels: 70.6 us -> 67.6 us
    pallas_call x1, Pallas kernels: 70.6 us -> 67.6 us  [local(): pl.pallas_call(head_kernel, out_shape=jax.ShapeDtypeStruct((15, 16, 80),...]
where the time goes in v2:
time: 69.2 us; the launch traced here: 69 us
  Pallas kernels  67.6 us (98%)
  local copies, waits for them, and re-layouts  1.46 us (2%)
    pallas_call x1, Pallas kernels, local(): pl.pallas_call(head_kernel, out_shape=jax.ShapeDtypeStruct((15, 16, 80),...  67.6 us
    unnamed x1, local copies, waits for them, and re-layouts  1.46 us

profile of v2, /device:TPU:1, one launch (start us, length us, event | category | flops | bytes accessed | tf_op | source)
XLA Modules:
  0.0 69.0 jit_solution(8321702066692286157)
XLA Ops:
  0.0 67.6 %aspp_head.1 = bf16[15,16,80]{2,1,0:T(8,128)(2,1)} custom-call(bf16[15,80,128]{2,1,0:T(8,128)(2,1)} %bitcast.4, bf16[128,256]{1,0:T(8,128)(2,1)} %pw.1, bf16[3,9,128,256]{3,2,1,0:T(8,128)(2,1)} %bitcast.3, bf16[128,256]{1,0:T(8,128)(2,1)} %wpool.1, bf16[1280,256]{1,0:T(8,128)(2,1)} %wproj.1, f32[6,256]{1,0:T(8,128)} %gain.1, f32[6,256]{1,0:T(8,128)} %shift.1), custom_call_target="tpu_custom_call" | custom-call | tf_op jit(solution)/shard_map/aspp_head/pallas_call | solution.py:334
  67.6 1.5 %copy.9 = bf16[80,15,16]{0,2,1:T(8,128)(2,1)} copy(bf16[80,15,16]{0,2,1:T(8,128)(2,1)} %bitcast.5) | data formatting | bytes 76800

commit v3 on v2

--- a/solution.py
+++ b/solution.py
@@ -36,13 +36,14 @@
         return ((zz % 8) * 4 + y, (zz // 8) * 8 + x * 2 + c)
 
     bit = ((z + 12) % 16) // 8
-    k = c * 8 + x * 2 + bit
-    kq, kt = k // 3, k % 3
+    zl_dst = (zl + 4) % 8
+    k = bit * 8 + x * 2 + c
+    kj, kt = k // 3, k % 3
+    kq = jnp.where(zl_dst == 0, 4 - kj, kj)
     kg = 4 * kq + y
     y_dst = kg // 5
     slot = (kg % 5) * 3 + kt
     has_col = k < 15
-    zl_dst = (zl + 4) % 8
 
     loads = [
         pltpu.make_async_copy(feat, xin, ld_sem.at[0]),
@@ -66,9 +67,9 @@
 
     def greet(i, carry):
         g = 5 * y + i // 3
-        kk = (g // 4) * 3 + i % 3
-        zz = (zl + 4 + 8 * (kk % 2)) % 16
-        hello(((zz % 8) * 4 + g % 4, (zz // 8) * 8 + ((kk // 2) % 4) * 2 + kk // 8))
+        kk = jnp.where(zl == 0, 4 - g // 4, g // 4) * 3 + i % 3
+        zz = (zl + 4 + 8 * (kk // 8)) % 16
+        hello(((zz % 8) * 4 + g % 4, (zz // 8) * 8 + kk % 8))
         return carry
 
     lax.fori_loop(0, 15, greet, 0)
@@ -86,7 +87,7 @@
 
     lax.fori_loop(0, 11, clear, 0)
     for b in range(4):
-        part[b, 15] = jnp.zeros((80, 256), BF16)
+        part[b, 1, 1, 3] = jnp.zeros((80, 256), BF16)
 
     loads[0].wait()
 
@@ -177,99 +178,113 @@
                     jnp.concatenate(taps, axis=1), wav[b - 1].reshape(1152, 256),
                     preferred_element_type=F32,
                 )
-            part[b, pl.ds(3 * q, 3)] = res.astype(BF16).reshape(3, 80, 256)
+            res = res.astype(BF16).reshape(3, 80, 256)
+            for t in range(3):
+                s = 3 * j + t
+                part[b, s % 2, s // 8, (s // 2) % 4] = res[t]
             return carry
 
         lax.fori_loop(lo, hi, body, 0)
 
     core_copies, x_copies, z_copies = {}, {}, {}
 
-    def core_send(b):
+    def core_send(b, h):
         copy = remote(
-            part.at[b, pl.ds((1 - c) * 8, 8)], cbuf.at[b], cs.at[b], cr.at[b], at(c_=1 - c)
+            part.at[b, 1 - c, h], cbuf.at[b, h], cs.at[b, h], cr.at[b, h], at(c_=1 - c)
         )
         copy.start()
-        core_copies[b] = copy
-
-    def core_reduce(b):
-        core_copies[b].wait_recv()
+        core_copies[b, h] = copy
+
+    def core_reduce(b, h):
+        core_copies[b, h].wait_recv()
 
         def body(i, carry):
-            mine = part[b, c * 8 + i].astype(F32) + cbuf[b, i].astype(F32)
-            part[b, c * 8 + i] = mine.astype(BF16)
+            mine = part[b, c, h, i].astype(F32) + cbuf[b, h, i].astype(F32)
+            part[b, c, h, i] = mine.astype(BF16)
             return carry
 
-        lax.fori_loop(0, 8, body, 0)
-        x_copies[b] = []
-        for d in range(1, 4):
+        lax.fori_loop(0, 4, body, 0)
+        x_copies[b, h] = []
+        for d in (2, 1, 3):
             to = (x + d) % 4
             copy = remote(
-                part.at[b, pl.ds(c * 8 + to * 2, 2)], xbuf.at[b, d - 1],
-                xs.at[b, d - 1], xr.at[b, d - 1], at(x_=to),
+                part.at[b, c, h, to], xbuf.at[b, h, d - 1],
+                xs.at[b, h, d - 1], xr.at[b, h, d - 1], at(x_=to),
             )
             copy.start()
-            x_copies[b].append(copy)
-
-    def x_reduce(b):
-        for copy in x_copies[b]:
+            x_copies[b, h].append(copy)
+
+    def x_reduce(b, h):
+        for copy in x_copies[b, h]:
             copy.wait_recv()
-        for j in range(2):
-            t = part[b, c * 8 + x * 2 + j].astype(F32)
-            for d in range(3):
-                t = t + xbuf[b, d, j].astype(F32)
-            zsrc[b, j] = t.astype(BF16)
-        z_copies[b] = []
-        for way in range(2):
-            j = zh if way == 0 else 1 - zh
-            copy = remote(
-                zsrc.at[b, j], zbuf.at[b, way], zs.at[b, way], zr.at[b, way],
-                at_z(4) if way == 0 else at_z(12),
-            )
-            copy.start()
-            z_copies[b].append(copy)
+        t = part[b, c, h, x].astype(F32)
+        for d in range(3):
+            t = t + xbuf[b, h, d].astype(F32)
+        zsrc[b, h] = t.astype(BF16)
+        up = (zh == h).astype(jnp.int32)
+        z_copies[b, h] = remote(
+            zsrc.at[b, h], zbuf.at[b, 1 - up], zs.at[b, h], zr.at[b, 1 - up], at_z(12 - 8 * up)
+        )
+        z_copies[b, h].start()
 
     compute(0, 0, 5)
-    core_send(0)
+    core_send(0, 0)
+    core_send(0, 1)
     own = poolsrc[0] + pool_get(0) + pool_get(1) + pool_get(2)
     poolsrc[1] = own
     pool_send(poolsrc.at[1], 3, east)
     pool_send(poolsrc.at[1], 4, west)
-    core_reduce(0)
-    for b in range(1, 4):
-        halo_wait(b - 1, 1 - late)
-        compute(b, 0, 5 - b)
+    core_reduce(0, 0)
+    core_reduce(0, 1)
+    halo_wait(0, 1 - late)
+    compute(1, 0, 4)
+    core_send(1, 0)
+    halo_wait(1, 1 - late)
+    compute(2, 0, 3)
+    core_send(2, 0)
+    core_reduce(1, 0)
+    x_reduce(0, 0)
+    x_reduce(0, 1)
+    halo_wait(2, 1 - late)
+    compute(3, 0, 2)
+    core_reduce(2, 0)
+    x_reduce(1, 0)
     halo_wait(0, late)
+    compute(3, 2, 3)
+    core_send(3, 0)
     compute(1, 4, 5)
-    core_send(1)
-    x_reduce(0)
+    core_send(1, 1)
+    core_reduce(3, 0)
+    halo_wait(1, late)
+    compute(2, 3, 5)
+    core_send(2, 1)
+    core_reduce(1, 1)
+    x_reduce(2, 0)
     three = own + pool_get(3) + pool_get(4)
     pool_send(poolbuf.at[4], 5, west)
-    core_reduce(1)
-    halo_wait(1, late)
-    compute(2, 3, 5)
-    core_send(2)
-    x_reduce(1)
-    core_reduce(2)
     halo_wait(2, late)
-    compute(3, 2, 5)
-    core_send(3)
+    compute(3, 3, 5)
+    core_send(3, 1)
+    core_reduce(2, 1)
+    x_reduce(3, 0)
+    core_reduce(3, 1)
+    x_reduce(1, 1)
+    x_reduce(2, 1)
     four = three + pool_get(5)
     poolsrc[2] = four
     pool_send(poolsrc.at[2], 6, at_z(4))
     pool_send(poolsrc.at[2], 7, at_z(12))
-    x_reduce(2)
-    core_reduce(3)
+    x_reduce(3, 1)
     twelve = four + pool_get(6) + pool_get(7)
     pool_send(poolbuf.at[7], 8, at_z(12))
-    x_reduce(3)
-    all_z = twelve + pool_get(8)
-    poolsrc[3] = all_z
-    pool_send(poolsrc.at[3], 9, at(c_=1 - c))
     loads[3].wait()
 
     proj = jnp.zeros((80, 256), F32)
     for b in range(4):
         if b == 2:
+            all_z = twelve + pool_get(8)
+            poolsrc[3] = all_z
+            pool_send(poolsrc.at[3], 9, at(c_=1 - c))
             both = all_z + pool_get(9)
             poolsrc[4] = both
             for d in range(1, 4):
@@ -282,8 +297,10 @@
                 jnp.broadcast_to(pooled, (16, 256)), wprojv[pl.ds(1024, 256), :],
                 preferred_element_type=F32,
             )[0:1]
-        for copy in z_copies[b]:
-            copy.wait_recv()
+        for way in range(2):
+            remote(
+                zsrc.at[b, 0], zbuf.at[b, way], zs.at[b, 0], zr.at[b, way], at_z(4)
+            ).wait_recv()
         total = zbuf[b, 0].astype(F32) + zbuf[b, 1].astype(F32)
         act = jnp.maximum(total * gain[b : b + 1] + shift[b : b + 1], 0.0).astype(BF16)
         proj = proj + jnp.dot(act, wprojv[pl.ds(b * 256, 256), :], preferred_element_type=F32)
@@ -304,9 +321,8 @@
     lax.fori_loop(0, 16, out_send, 0)
     for copy in ycopies + halo + psends:
         copy.wait_send()
-    for b in range(4):
-        core_copies[b].wait_send()
-        for copy in x_copies[b] + z_copies[b]:
+    for u in core_copies:
+        for copy in [core_copies[u], z_copies[u]] + x_copies[u]:
             copy.wait_send()
 
     def out_recv(i, carry):
@@ -339,9 +355,9 @@
         scratch_shapes=[
             pltpu.VMEM((15, 80, 128), BF16),
             pltpu.VMEM((11, 3, 80 + 2 * PAD, 128), BF16),
-            pltpu.VMEM((4, 16, 80, 256), BF16),
-            pltpu.VMEM((4, 8, 80, 256), BF16),
-            pltpu.VMEM((4, 3, 2, 80, 256), BF16),
+            pltpu.VMEM((4, 2, 2, 4, 80, 256), BF16),
+            pltpu.VMEM((4, 2, 4, 80, 256), BF16),
+            pltpu.VMEM((4, 2, 3, 80, 256), BF16),
             pltpu.VMEM((4, 2, 80, 256), BF16),
             pltpu.VMEM((4, 2, 80, 256), BF16),
             pltpu.VMEM((16, 16, 128), BF16),
@@ -354,8 +370,8 @@
             dma((4,)),
             dma((3,)), dma((3,)),
             dma((6,)), dma((6,)),
-            dma((4,)), dma((4,)),
-            dma((4, 3)), dma((4, 3)),
+            dma((4, 2)), dma((4, 2)),
+            dma((4, 2, 3)), dma((4, 2, 3)),
             dma((4, 2)), dma((4, 2)),
             dma((16,)), dma((15,)),
             dma((13,)), dma((13,)),

time: 69.2 us -> 77.3 us (1.12)
  Pallas kernels: 67.6 us -> 75.6 us
    pallas_call x1, Pallas kernels: 67.6 us -> 75.6 us  [local(): pl.pallas_call(head_kernel, out_shape=jax.ShapeDtypeStruct((15, 16, 80),...]
where the time goes in v3:
time: 77.3 us; the launch traced here: 77.1 us
  Pallas kernels  75.6 us (98%)
  local copies, waits for them, and re-layouts  1.46 us (2%)
    pallas_call x1, Pallas kernels, local(): pl.pallas_call(head_kernel, out_shape=jax.ShapeDtypeStruct((15, 16, 80),...  75.6 us

profile of v3, /device:TPU:1, one launch (start us, length us, event | category | flops | bytes accessed | tf_op | source)
XLA Modules:
  0.0 77.1 jit_solution(7575567677820321797)
XLA Ops:
  0.0 75.6 %aspp_head.1 = bf16[15,16,80]{2,1,0:T(8,128)(2,1)} custom-call(bf16[15,80,128]{2,1,0:T(8,128)(2,1)} %bitcast.4, bf16[128,256]{1,0:T(8,128)(2,1)} %pw.1, bf16[3,9,128,256]{3,2,1,0:T(8,128)(2,1)} %bitcast.3, bf16[128,256]{1,0:T(8,128)(2,1)} %wpool.1, bf16[1280,256]{1,0:T(8,128)(2,1)} %wproj.1, f32[6,256]{1,0:T(8,128)} %gain.1, f32[6,256]{1,0:T(8,128)} %shift.1), custom_call_target="tpu_custom_call" | custom-call | tf_op jit(solution)/shard_map/aspp_head/pallas_call | solution.py:350
  75.6 1.5 %copy.9 = bf16[80,15,16]{0,2,1:T(8,128)(2,1)} copy(bf16[80,15,16]{0,2,1:T(8,128)(2,1)} %bitcast.5) | data formatting | bytes 76800

commit v4 on v3

--- a/solution.py
+++ b/solution.py
@@ -16,7 +16,9 @@
     feat, pw, wa, wpool, wproj, gain, shift, out,
     xin, xb, part, cbuf, xbuf, zsrc, zbuf, stage, obuf,
     pwv, wav, wprojv, poolsrc, poolbuf,
+    part2, cbuf2, xbuf2, zsrc2, zbuf2, acc,
     ld_sem, ys, yr, hs, hr, cs, cr, xs, xr, zs, zr, os, orr, ps, pr,
+    cs2, cr2, xs2, xr2, zs2, zr2,
 ):
     lon = lax.axis_index("lon")
     ch = lax.axis_index("ch")
@@ -60,8 +62,23 @@
         pl.semaphore_signal(barrier, inc=1, device_id=dev, device_id_type=MESH_ID)
 
     east, west = at(zl_=(zl + 1) % 8), at(zl_=(zl + 7) % 8)
-    hello(east)
-    hello(west)
+    edge = jnp.logical_or(zl == 0, zl == 7)
+    edge_owner = jnp.logical_or(zl == 3, zl == 4)
+
+    @pl.when(edge_owner)
+    def _():
+        far = jnp.where(zl == 4, 7, 0) * 4 + y
+        hello((far, x * 2 + c))
+        hello((far, 8 + x * 2 + c))
+
+    @pl.when(zl < 7)
+    def _():
+        hello(east)
+
+    @pl.when(zl > 0)
+    def _():
+        hello(west)
+
     hello(at_z(4))
     hello(at_z(12))
 
@@ -89,20 +106,30 @@
     for b in range(4):
         part[b, 1, 1, 3] = jnp.zeros((80, 256), BF16)
 
+    blank = jnp.zeros((3, 80, 128), BF16)
+
+    @pl.when(edge)
+    def _():
+        for d in range(3):
+            xb[jnp.where(zl == 0, d, 8 + d), :, pl.ds(PAD, 80), :] = blank
+        part2[1, 0, 1, 0] = jnp.zeros((80, 256), BF16)
+        for b in range(3):
+            part2[b, 1, 1, 3] = jnp.zeros((80, 256), BF16)
+
     loads[0].wait()
 
-    def add_col(i, acc):
-        return acc + jnp.sum(xin[i].astype(F32).reshape(10, 8, 128), axis=0)
-
-    acc = lax.fori_loop(0, 15, add_col, jnp.zeros((8, 128), F32))
-    colsum = jnp.sum(acc, axis=0, keepdims=True)
+    def add_col(i, tot):
+        return tot + jnp.sum(xin[i].astype(F32).reshape(10, 8, 128), axis=0)
+
+    sums = lax.fori_loop(0, 15, add_col, jnp.zeros((8, 128), F32))
+    colsum = jnp.sum(sums, axis=0, keepdims=True)
     pre = jnp.dot(
         jnp.broadcast_to(colsum, (8, 128)), wpool[...].astype(F32),
         precision=lax.Precision.HIGHEST, preferred_element_type=F32,
     )[0:1]
     poolsrc[0] = pre
 
-    pl.semaphore_wait(barrier, 11 + 16 * has_col.astype(jnp.int32))
+    pl.semaphore_wait(barrier, 11 + edge.astype(jnp.int32) + 16 * has_col.astype(jnp.int32))
 
     def remote(src, dst, ssem, rsem, dev):
         return pltpu.make_async_remote_copy(
@@ -120,12 +147,11 @@
         )
         copy.start()
         ycopies.append(copy)
-    psends = []
+    psends = {}
 
     def pool_send(src, slot_i, dev):
-        copy = remote(src, poolbuf.at[slot_i], ps.at[slot_i], pr.at[slot_i], dev)
-        copy.start()
-        psends.append(copy)
+        psends[slot_i] = remote(src, poolbuf.at[slot_i], ps.at[slot_i], pr.at[slot_i], dev)
+        psends[slot_i].start()
 
     def pool_get(slot_i):
         psends[slot_i].wait_recv()
@@ -138,26 +164,30 @@
     for copy in ycopies:
         copy.wait_recv()
 
-    halo = []
+    def halo_copy(d, side):
+        q = (4 - d) if side == 0 else d
+        q_to = q - 5 if side == 0 else q + 5
+        return remote(
+            xb.at[q + 3, :, rows, :], xb.at[q_to + 3, :, rows, :],
+            hs.at[2 * d + side], hr.at[2 * d + side], east if side == 0 else west,
+        )
+
+    halo_out = (zl < 7, zl > 0)
+    halo_in = (zl > 0, zl < 7)
     for d in range(3):
         for side in range(2):
-            q = (4 - d) if side == 0 else d
-            q_to = q - 5 if side == 0 else q + 5
-            copy = remote(
-                xb.at[q + 3, :, rows, :], xb.at[q_to + 3, :, rows, :],
-                hs.at[2 * d + side], hr.at[2 * d + side], east if side == 0 else west,
-            )
-            copy.start()
-            halo.append(copy)
+            pl.when(halo_out[side])(halo_copy(d, side).start)
+
+    def halo_wait(d):
+        for side in range(2):
+            pl.when(halo_in[side])(halo_copy(d, side).wait_recv)
 
     late = jnp.where(zl == 0, 0, 1)
 
-    def halo_wait(d, side):
-        remote(
-            xb.at[3, :, rows, :], xb.at[4, :, rows, :],
-            hs.at[2 * d + side], hr.at[2 * d + side], east,
-        ).wait_recv()
-
+    own = poolsrc[0] + pool_get(0) + pool_get(1) + pool_get(2)
+    poolsrc[1] = own
+    pool_send(poolsrc.at[1], 3, at_z(4))
+    pool_send(poolsrc.at[1], 4, at_z(12))
     loads[1].wait()
     loads[2].wait()
 
@@ -227,68 +257,169 @@
         )
         z_copies[b, h].start()
 
+    extra = ((3, 0, 3), (3, 1, 0), (2, 1, 0), (1, 1, 2))
+
+    def extra_compute(b):
+        col = jnp.where(zl == 7, 0, 2)
+        kernel = jnp.concatenate([wav[b - 1, r * 3 + col] for r in range(3)], axis=0)
+
+        def body(j, carry):
+            q = jnp.where(zl == 7, 9 - j - b, j + b - 5)
+            lhs = jnp.concatenate(
+                [
+                    xb[q + 3, :, pl.ds(PAD + ro * b * 12, 80), :].reshape(240, 128)
+                    for ro in (-1, 0, 1)
+                ],
+                axis=1,
+            )
+            res = jnp.dot(lhs, kernel, preferred_element_type=F32)
+            res = res.astype(BF16).reshape(3, 80, 256)
+            for t in range(3):
+                s = 3 * j + t
+                part2[b - 1, s % 2, s // 8, (s // 2) % 4] = res[t]
+            return carry
+
+        lax.fori_loop(5 - b, 5, body, 0)
+
+    def extra_core(b, h, lo):
+        n = 4 - lo
+        return remote(
+            part2.at[b - 1, 1 - c, h, pl.ds(lo, n)], cbuf2.at[b - 1, h, pl.ds(lo, n)],
+            cs2.at[b - 1, h], cr2.at[b - 1, h], at(c_=1 - c),
+        )
+
+    def extra_x(b, h, d):
+        to = (x + d) % 4
+        return remote(
+            part2.at[b - 1, c, h, to], xbuf2.at[b - 1, h, d - 1],
+            xs2.at[b - 1, h, d - 1], xr2.at[b - 1, h, d - 1], at(x_=to),
+        )
+
+    def extra_z(b, h):
+        zz = (7 - zl + 4 + 8 * h) % 16
+        return remote(
+            zsrc2.at[b - 1, h], zbuf2.at[b - 1, zh], zs2.at[b - 1, h], zr2.at[b - 1, zh],
+            ((zz % 8) * 4 + y, (zz // 8) * 8 + x * 2 + c),
+        )
+
+    def extra_core_reduce(b, h, lo):
+        extra_core(b, h, lo).wait_recv()
+        for i in range(lo, 4):
+            mine = part2[b - 1, c, h, i].astype(F32) + cbuf2[b - 1, h, i].astype(F32)
+            part2[b - 1, c, h, i] = mine.astype(BF16)
+        for d in (2, 1, 3):
+            pl.when((x + d) % 4 >= lo)(extra_x(b, h, d).start)
+
+    def extra_x_reduce(b, h, lo):
+        @pl.when(x >= lo)
+        def _():
+            t = part2[b - 1, c, h, x].astype(F32)
+            for d in (2, 1, 3):
+                extra_x(b, h, d).wait_recv()
+                t = t + xbuf2[b - 1, h, d - 1].astype(F32)
+            zsrc2[b - 1, h] = t.astype(BF16)
+            extra_z(b, h).start()
+
+    def extra_sent(b, h, lo):
+        extra_core(b, h, lo).wait_send()
+        for d in (2, 1, 3):
+            pl.when((x + d) % 4 >= lo)(extra_x(b, h, d).wait_send)
+        pl.when(x >= lo)(extra_z(b, h).wait_send)
+
     compute(0, 0, 5)
     core_send(0, 0)
     core_send(0, 1)
-    own = poolsrc[0] + pool_get(0) + pool_get(1) + pool_get(2)
-    poolsrc[1] = own
-    pool_send(poolsrc.at[1], 3, east)
-    pool_send(poolsrc.at[1], 4, west)
+
+    @pl.when(edge)
+    def _():
+        extra_compute(3)
+        extra_core(*extra[0]).start()
+        extra_core(*extra[1]).start()
+        extra_compute(2)
+        extra_core(*extra[2]).start()
+        extra_compute(1)
+        extra_core(*extra[3]).start()
+
     core_reduce(0, 0)
     core_reduce(0, 1)
-    halo_wait(0, 1 - late)
-    compute(1, 0, 4)
+
+    @pl.when(edge)
+    def _():
+        for u in extra:
+            extra_core_reduce(*u)
+
+    halo_wait(0)
+    compute(1, 0, 5)
     core_send(1, 0)
-    halo_wait(1, 1 - late)
-    compute(2, 0, 3)
+    core_send(1, 1)
+    three = own + pool_get(3) + pool_get(4)
+    pool_send(poolbuf.at[4], 5, at_z(12))
+    halo_wait(1)
+    compute(2, 0, 5)
     core_send(2, 0)
+    core_send(2, 1)
     core_reduce(1, 0)
+    core_reduce(1, 1)
     x_reduce(0, 0)
     x_reduce(0, 1)
-    halo_wait(2, 1 - late)
-    compute(3, 0, 2)
+    halo_wait(2)
+    compute(3, 0, 5)
+    core_send(3, 0)
+    core_send(3, 1)
     core_reduce(2, 0)
-    x_reduce(1, 0)
-    halo_wait(0, late)
-    compute(3, 2, 3)
-    core_send(3, 0)
-    compute(1, 4, 5)
-    core_send(1, 1)
-    core_reduce(3, 0)
-    halo_wait(1, late)
-    compute(2, 3, 5)
-    core_send(2, 1)
-    core_reduce(1, 1)
-    x_reduce(2, 0)
-    three = own + pool_get(3) + pool_get(4)
-    pool_send(poolbuf.at[4], 5, west)
-    halo_wait(2, late)
-    compute(3, 3, 5)
-    core_send(3, 1)
     core_reduce(2, 1)
-    x_reduce(3, 0)
-    core_reduce(3, 1)
-    x_reduce(1, 1)
-    x_reduce(2, 1)
     four = three + pool_get(5)
     poolsrc[2] = four
-    pool_send(poolsrc.at[2], 6, at_z(4))
-    pool_send(poolsrc.at[2], 7, at_z(12))
+    pool_send(poolsrc.at[2], 6, at(zl_=zl + 1 - 2 * (zl % 2)))
+
+    @pl.when(edge)
+    def _():
+        for u in extra:
+            extra_x_reduce(*u)
+
+    x_reduce(1, 0)
+    x_reduce(1, 1)
+    core_reduce(3, 0)
+    core_reduce(3, 1)
+
+    pair = four + pool_get(6)
+    poolsrc[3] = pair
+    place = zl % 4
+    middle = jnp.logical_or(place == 1, place == 2)
+
+    def pool_copy(src, slot_i, dev):
+        return remote(poolsrc.at[src], poolbuf.at[slot_i], ps.at[slot_i], pr.at[slot_i], dev)
+
+    inward = pool_copy(3, 7, at(zl_=(zl + jnp.where(place == 1, 1, 7)) % 8))
+    outward = pool_copy(4, 8, at(zl_=(zl + jnp.where(place == 1, 7, 1)) % 8))
+    pl.when(middle)(inward.start)
+    x_reduce(2, 0)
+    x_reduce(2, 1)
+
+    @pl.when(middle)
+    def _():
+        inward.wait_recv()
+        poolsrc[4] = poolsrc[3] + poolbuf[7]
+        outward.start()
+
+    x_reduce(3, 0)
     x_reduce(3, 1)
-    twelve = four + pool_get(6) + pool_get(7)
-    pool_send(poolbuf.at[7], 8, at_z(12))
+
+    @pl.when(jnp.logical_not(middle))
+    def _():
+        outward.wait_recv()
+        poolsrc[4] = poolbuf[8]
+
+    pool_send(poolsrc.at[4], 9, at(c_=1 - c))
     loads[3].wait()
 
     proj = jnp.zeros((80, 256), F32)
     for b in range(4):
-        if b == 2:
-            all_z = twelve + pool_get(8)
-            poolsrc[3] = all_z
-            pool_send(poolsrc.at[3], 9, at(c_=1 - c))
-            both = all_z + pool_get(9)
-            poolsrc[4] = both
+        if b == 1:
+            both = poolsrc[4] + pool_get(9)
+            poolsrc[5] = both
             for d in range(1, 4):
-                pool_send(poolsrc.at[4], 9 + d, at(x_=(x + d) % 4))
+                pool_send(poolsrc.at[5], 9 + d, at(x_=(x + d) % 4))
         if b == 3:
             pre_all = both + pool_get(10) + pool_get(11) + pool_get(12)
             pre_all = pre_all * (1.0 / 38400.0)
@@ -301,8 +432,22 @@
             remote(
                 zsrc.at[b, 0], zbuf.at[b, way], zs.at[b, 0], zr.at[b, way], at_z(4)
             ).wait_recv()
-        total = zbuf[b, 0].astype(F32) + zbuf[b, 1].astype(F32)
-        act = jnp.maximum(total * gain[b : b + 1] + shift[b : b + 1], 0.0).astype(BF16)
+        acc[b] = zbuf[b, 0].astype(F32) + zbuf[b, 1].astype(F32)
+        if b > 0:
+            over = jnp.logical_and(bit == 1, x >= (2 if b == 1 else 0))
+            if b == 3:
+                over = jnp.logical_or(over, jnp.logical_and(bit == 0, x == 3))
+
+            @pl.when(jnp.logical_and(edge_owner, over))
+            def _():
+                for half in range(2):
+                    remote(
+                        zsrc2.at[b - 1, 0], zbuf2.at[b - 1, half],
+                        zs2.at[b - 1, 0], zr2.at[b - 1, half], at_z(4),
+                    ).wait_recv()
+                acc[b] += zbuf2[b - 1, 0].astype(F32) + zbuf2[b - 1, 1].astype(F32)
+
+        act = jnp.maximum(acc[b] * gain[b : b + 1] + shift[b : b + 1], 0.0).astype(BF16)
         proj = proj + jnp.dot(act, wprojv[pl.ds(b * 256, 256), :], preferred_element_type=F32)
     head = jnp.maximum(gain[5:6] * (proj + pool_term) + shift[5:6], 0.0)
     head = jnp.concatenate([head, jnp.zeros((48, 256), F32)], axis=0)
@@ -319,8 +464,22 @@
         return carry
 
     lax.fori_loop(0, 16, out_send, 0)
-    for copy in ycopies + halo + psends:
+    for copy in ycopies + list(psends.values()):
         copy.wait_send()
+    for d in range(3):
+        for side in range(2):
+            pl.when(halo_out[side])(halo_copy(d, side).wait_send)
+
+    @pl.when(middle)
+    def _():
+        inward.wait_send()
+        outward.wait_send()
+
+    @pl.when(edge)
+    def _():
+        for u in extra:
+            extra_sent(*u)
+
     for u in core_copies:
         for copy in [core_copies[u], z_copies[u]] + x_copies[u]:
             copy.wait_send()
@@ -365,8 +524,14 @@
             pltpu.VMEM((128, 256), BF16),
             pltpu.VMEM((3, 9, 128, 256), BF16),
             pltpu.VMEM((1280, 256), BF16),
-            pltpu.VMEM((5, 1, 256), F32),
+            pltpu.VMEM((6, 1, 256), F32),
             pltpu.VMEM((13, 1, 256), F32),
+            pltpu.VMEM((3, 2, 2, 4, 80, 256), BF16),
+            pltpu.VMEM((3, 2, 4, 80, 256), BF16),
+            pltpu.VMEM((3, 2, 3, 80, 256), BF16),
+            pltpu.VMEM((3, 2, 80, 256), BF16),
+            pltpu.VMEM((3, 2, 80, 256), BF16),
+            pltpu.VMEM((4, 80, 256), F32),
             dma((4,)),
             dma((3,)), dma((3,)),
             dma((6,)), dma((6,)),
@@ -375,6 +540,9 @@
             dma((4, 2)), dma((4, 2)),
             dma((16,)), dma((15,)),
             dma((13,)), dma((13,)),
+            dma((3, 2)), dma((3, 2)),
+            dma((3, 2, 3)), dma((3, 2, 3)),
+            dma((3, 2)), dma((3, 2)),
         ],
         compiler_params=pltpu.CompilerParams(collective_id=0, has_side_effects=True),
         name="aspp_head",

time: 77.3 us -> 67.1 us (0.87)
  Pallas kernels: 75.6 us -> 65.4 us
    pallas_call x1, Pallas kernels: 75.6 us -> 65.4 us  [local(): pl.pallas_call(head_kernel, out_shape=jax.ShapeDtypeStruct((15, 16, 80),...]
where the time goes in v4:
time: 67.1 us; the launch traced here: 66.9 us
  Pallas kernels  65.4 us (97%)
  local copies, waits for them, and re-layouts  1.46 us (2%)
    pallas_call x1, Pallas kernels, local(): pl.pallas_call(head_kernel, out_shape=jax.ShapeDtypeStruct((15, 16, 80),...  65.4 us
    unnamed x1, local copies, waits for them, and re-layouts  1.46 us

profile of v4, /device:TPU:1, one launch (start us, length us, event | category | flops | bytes accessed | tf_op | source)
XLA Modules:
  0.0 66.9 jit_solution(15733835429242415090)
XLA Ops:
  0.0 65.4 %aspp_head.1 = bf16[15,16,80]{2,1,0:T(8,128)(2,1)} custom-call(bf16[15,80,128]{2,1,0:T(8,128)(2,1)} %bitcast.4, bf16[128,256]{1,0:T(8,128)(2,1)} %pw.1, bf16[3,9,128,256]{3,2,1,0:T(8,128)(2,1)} %bitcast.3, bf16[128,256]{1,0:T(8,128)(2,1)} %wpool.1, bf16[1280,256]{1,0:T(8,128)(2,1)} %wproj.1, f32[6,256]{1,0:T(8,128)} %gain.1, f32[6,256]{1,0:T(8,128)} %shift.1), custom_call_target="tpu_custom_call" | custom-call | tf_op jit(solution)/shard_map/aspp_head/pallas_call | solution.py:509
  65.4 1.5 %copy.9 = bf16[80,15,16]{0,2,1:T(8,128)(2,1)} copy(bf16[80,15,16]{0,2,1:T(8,128)(2,1)} %bitcast.5) | data formatting | bytes 76800

commit v5 on v4

--- a/solution.py
+++ b/solution.py
@@ -16,7 +16,7 @@
     feat, pw, wa, wpool, wproj, gain, shift, out,
     xin, xb, part, cbuf, xbuf, zsrc, zbuf, stage, obuf,
     pwv, wav, wprojv, poolsrc, poolbuf,
-    part2, cbuf2, xbuf2, zsrc2, zbuf2, acc,
+    part2, cbuf2, xbuf2, zsrc2, zbuf2, acc, xacc,
     ld_sem, ys, yr, hs, hr, cs, cr, xs, xr, zs, zr, os, orr, ps, pr,
     cs2, cr2, xs2, xr2, zs2, zr2,
 ):
@@ -37,11 +37,15 @@
         zz = (z + dz) % 16
         return ((zz % 8) * 4 + y, (zz // 8) * 8 + x * 2 + c)
 
+    def block_of(j, level):
+        q = (j + 1) % 5
+        return jnp.where(level == 0, 4 - q, q)
+
     bit = ((z + 12) % 16) // 8
     zl_dst = (zl + 4) % 8
     k = bit * 8 + x * 2 + c
     kj, kt = k // 3, k % 3
-    kq = jnp.where(zl_dst == 0, 4 - kj, kj)
+    kq = block_of(kj, zl_dst)
     kg = 4 * kq + y
     y_dst = kg // 5
     slot = (kg % 5) * 3 + kt
@@ -82,14 +86,6 @@
     hello(at_z(4))
     hello(at_z(12))
 
-    def greet(i, carry):
-        g = 5 * y + i // 3
-        kk = jnp.where(zl == 0, 4 - g // 4, g // 4) * 3 + i % 3
-        zz = (zl + 4 + 8 * (kk // 8)) % 16
-        hello(((zz % 8) * 4 + g % 4, (zz // 8) * 8 + kk % 8))
-        return carry
-
-    lax.fori_loop(0, 15, greet, 0)
     for d in range(1, 4):
         hello(at(y_=(y + d) % 4))
         hello(at(x_=(x + d) % 4))
@@ -112,11 +108,12 @@
     def _():
         for d in range(3):
             xb[jnp.where(zl == 0, d, 8 + d), :, pl.ds(PAD, 80), :] = blank
-        part2[1, 0, 1, 0] = jnp.zeros((80, 256), BF16)
-        for b in range(3):
-            part2[b, 1, 1, 3] = jnp.zeros((80, 256), BF16)
+        part2[0, 0, 1, 0] = jnp.zeros((80, 256), BF16)
+        part2[2, 0, 0, 1] = jnp.zeros((80, 256), BF16)
 
     loads[0].wait()
+    xb[y + 3, :, pl.ds(PAD, 80), :] = xin[0:3]
+    xb[y + 4, :, pl.ds(PAD, 80), :] = xin[12:15]
 
     def add_col(i, tot):
         return tot + jnp.sum(xin[i].astype(F32).reshape(10, 8, 128), axis=0)
@@ -129,7 +126,7 @@
     )[0:1]
     poolsrc[0] = pre
 
-    pl.semaphore_wait(barrier, 11 + edge.astype(jnp.int32) + 16 * has_col.astype(jnp.int32))
+    pl.semaphore_wait(barrier, 11 + edge.astype(jnp.int32))
 
     def remote(src, dst, ssem, rsem, dev):
         return pltpu.make_async_remote_copy(
@@ -159,10 +156,6 @@
 
     for d in range(1, 4):
         pool_send(poolsrc.at[0], d - 1, at(y_=(y + d) % 4))
-    xb[y + 3, :, rows, :] = xin[0:3]
-    xb[y + 4, :, rows, :] = xin[12:15]
-    for copy in ycopies:
-        copy.wait_recv()
 
     def halo_copy(d, side):
         q = (4 - d) if side == 0 else d
@@ -174,26 +167,30 @@
 
     halo_out = (zl < 7, zl > 0)
     halo_in = (zl > 0, zl < 7)
-    for d in range(3):
-        for side in range(2):
+    for d, sides in ((0, (0,)), (0, (1,)), (1, (0,)), (1, (1,)), (2, (0, 1))):
+        q = (4 - d) if sides[0] == 0 else d
+        g = (4 * q + y) % 5
+
+        @pl.when(jnp.logical_and(g > 0, g < 4))
+        def _():
+            gi = jnp.clip(g - 1, 0, 2)
+            remote(
+                xin.at[pl.ds(0, 3)], xb.at[q + 3, :, rows, :], ys.at[gi], yr.at[gi], east
+            ).wait_recv()
+
+        for side in sides:
             pl.when(halo_out[side])(halo_copy(d, side).start)
 
     def halo_wait(d):
         for side in range(2):
             pl.when(halo_in[side])(halo_copy(d, side).wait_recv)
 
-    late = jnp.where(zl == 0, 0, 1)
-
-    own = poolsrc[0] + pool_get(0) + pool_get(1) + pool_get(2)
-    poolsrc[1] = own
-    pool_send(poolsrc.at[1], 3, at_z(4))
-    pool_send(poolsrc.at[1], 4, at_z(12))
     loads[1].wait()
     loads[2].wait()
 
     def compute(b, lo, hi):
         def body(j, carry):
-            q = jnp.where(late == 1, j, 4 - j)
+            q = block_of(j, zl)
             if b == 0:
                 lhs = xb[q + 3, :, rows, :].reshape(240, 128)
                 res = jnp.dot(lhs, pwv[...], preferred_element_type=F32)
@@ -234,37 +231,52 @@
             return carry
 
         lax.fori_loop(0, 4, body, 0)
+        first = flip if h == 0 else 3 - x
         x_copies[b, h] = []
-        for d in (2, 1, 3):
-            to = (x + d) % 4
+        for i, col in enumerate((first, (x + 2) % 4)):
             copy = remote(
-                part.at[b, c, h, to], xbuf.at[b, h, d - 1],
-                xs.at[b, h, d - 1], xr.at[b, h, d - 1], at(x_=to),
+                part.at[b, c, h, col], xbuf.at[b, h, i], xs.at[b, h, i], xr.at[b, h, i],
+                at(x_=first),
             )
             copy.start()
             x_copies[b, h].append(copy)
 
-    def x_reduce(b, h):
+    flip = x + 1 - 2 * (x % 2)
+
+    def x_half(b, h):
+        second = 3 - x if h == 0 else flip
         for copy in x_copies[b, h]:
             copy.wait_recv()
-        t = part[b, c, h, x].astype(F32)
-        for d in range(3):
-            t = t + xbuf[b, h, d].astype(F32)
-        zsrc[b, h] = t.astype(BF16)
+        give = part[b, c, h, second].astype(F32) + xbuf[b, h, 1].astype(F32)
+        part[b, c, h, second] = give.astype(BF16)
+        copy = remote(
+            part.at[b, c, h, second], xbuf.at[b, h, 2], xs.at[b, h, 2], xr.at[b, h, 2],
+            at(x_=second),
+        )
+        copy.start()
+        x_copies[b, h].append(copy)
+        xacc[b, h] = part[b, c, h, x].astype(F32) + xbuf[b, h, 0].astype(F32)
+
+    def x_reduce(b, h):
+        x_copies[b, h][2].wait_recv()
+        zsrc[b, h] = (xacc[b, h] + xbuf[b, h, 2].astype(F32)).astype(BF16)
         up = (zh == h).astype(jnp.int32)
         z_copies[b, h] = remote(
             zsrc.at[b, h], zbuf.at[b, 1 - up], zs.at[b, h], zr.at[b, 1 - up], at_z(12 - 8 * up)
         )
         z_copies[b, h].start()
 
-    extra = ((3, 0, 3), (3, 1, 0), (2, 1, 0), (1, 1, 2))
+    extra = ((3, 0, 1, 4), (3, 1, 0, 2), (2, 0, 3, 4), (2, 1, 0, 2), (1, 1, 0, 2))
+
+    def within(to, lo, hi):
+        return jnp.logical_and(to >= lo, to < hi)
 
     def extra_compute(b):
         col = jnp.where(zl == 7, 0, 2)
         kernel = jnp.concatenate([wav[b - 1, r * 3 + col] for r in range(3)], axis=0)
 
         def body(j, carry):
-            q = jnp.where(zl == 7, 9 - j - b, j + b - 5)
+            q = jnp.where(zl == 7, 8 - j - b, j + b - 4)
             lhs = jnp.concatenate(
                 [
                     xb[q + 3, :, pl.ds(PAD + ro * b * 12, 80), :].reshape(240, 128)
@@ -279,10 +291,10 @@
                 part2[b - 1, s % 2, s // 8, (s // 2) % 4] = res[t]
             return carry
 
-        lax.fori_loop(5 - b, 5, body, 0)
-
-    def extra_core(b, h, lo):
-        n = 4 - lo
+        lax.fori_loop(4 - b, 4, body, 0)
+
+    def extra_core(b, h, lo, hi):
+        n = hi - lo
         return remote(
             part2.at[b - 1, 1 - c, h, pl.ds(lo, n)], cbuf2.at[b - 1, h, pl.ds(lo, n)],
             cs2.at[b - 1, h], cr2.at[b - 1, h], at(c_=1 - c),
@@ -302,16 +314,16 @@
             ((zz % 8) * 4 + y, (zz // 8) * 8 + x * 2 + c),
         )
 
-    def extra_core_reduce(b, h, lo):
-        extra_core(b, h, lo).wait_recv()
-        for i in range(lo, 4):
+    def extra_core_reduce(b, h, lo, hi):
+        extra_core(b, h, lo, hi).wait_recv()
+        for i in range(lo, hi):
             mine = part2[b - 1, c, h, i].astype(F32) + cbuf2[b - 1, h, i].astype(F32)
             part2[b - 1, c, h, i] = mine.astype(BF16)
         for d in (2, 1, 3):
-            pl.when((x + d) % 4 >= lo)(extra_x(b, h, d).start)
-
-    def extra_x_reduce(b, h, lo):
-        @pl.when(x >= lo)
+            pl.when(within((x + d) % 4, lo, hi))(extra_x(b, h, d).start)
+
+    def extra_x_reduce(b, h, lo, hi):
+        @pl.when(within(x, lo, hi))
         def _():
             t = part2[b - 1, c, h, x].astype(F32)
             for d in (2, 1, 3):
@@ -320,15 +332,24 @@
             zsrc2[b - 1, h] = t.astype(BF16)
             extra_z(b, h).start()
 
-    def extra_sent(b, h, lo):
-        extra_core(b, h, lo).wait_send()
+    def extra_sent(b, h, lo, hi):
+        extra_core(b, h, lo, hi).wait_send()
         for d in (2, 1, 3):
-            pl.when((x + d) % 4 >= lo)(extra_x(b, h, d).wait_send)
-        pl.when(x >= lo)(extra_z(b, h).wait_send)
-
-    compute(0, 0, 5)
+            pl.when(within((x + d) % 4, lo, hi))(extra_x(b, h, d).wait_send)
+        pl.when(within(x, lo, hi))(extra_z(b, h).wait_send)
+
+    compute(0, 0, 3)
     core_send(0, 0)
+    compute(0, 3, 5)
     core_send(0, 1)
+    compute(1, 0, 3)
+    core_send(1, 0)
+    own = poolsrc[0] + pool_get(0) + pool_get(1) + pool_get(2)
+    poolsrc[1] = own
+    pool_send(poolsrc.at[1], 3, at_z(4))
+    pool_send(poolsrc.at[1], 4, at_z(12))
+    core_reduce(0, 0)
+    core_reduce(0, 1)
 
     @pl.when(edge)
     def _():
@@ -337,37 +358,45 @@
         extra_core(*extra[1]).start()
         extra_compute(2)
         extra_core(*extra[2]).start()
+        extra_core(*extra[3]).start()
         extra_compute(1)
-        extra_core(*extra[3]).start()
-
-    core_reduce(0, 0)
-    core_reduce(0, 1)
+        extra_core(*extra[4]).start()
+
+    core_reduce(1, 0)
+    halo_wait(0)
+    compute(2, 0, 3)
+    core_send(2, 0)
+    compute(1, 3, 5)
+    core_send(1, 1)
 
     @pl.when(edge)
     def _():
         for u in extra:
             extra_core_reduce(*u)
 
-    halo_wait(0)
-    compute(1, 0, 5)
-    core_send(1, 0)
-    core_send(1, 1)
+    x_half(0, 0)
+    x_half(0, 1)
+    core_reduce(2, 0)
+    core_reduce(1, 1)
+    halo_wait(1)
+    compute(3, 0, 3)
+    core_send(3, 0)
+    compute(2, 3, 5)
+    core_send(2, 1)
     three = own + pool_get(3) + pool_get(4)
     pool_send(poolbuf.at[4], 5, at_z(12))
-    halo_wait(1)
-    compute(2, 0, 5)
-    core_send(2, 0)
-    core_send(2, 1)
-    core_reduce(1, 0)
-    core_reduce(1, 1)
     x_reduce(0, 0)
     x_reduce(0, 1)
+    x_half(1, 0)
+    core_reduce(3, 0)
+    core_reduce(2, 1)
     halo_wait(2)
-    compute(3, 0, 5)
-    core_send(3, 0)
+    compute(3, 3, 5)
     core_send(3, 1)
-    core_reduce(2, 0)
-    core_reduce(2, 1)
+    x_half(2, 0)
+    x_half(1, 1)
+    x_reduce(1, 0)
+    core_reduce(3, 1)
     four = three + pool_get(5)
     poolsrc[2] = four
     pool_send(poolsrc.at[2], 6, at(zl_=zl + 1 - 2 * (zl % 2)))
@@ -377,10 +406,10 @@
         for u in extra:
             extra_x_reduce(*u)
 
-    x_reduce(1, 0)
+    x_half(3, 0)
+    x_half(2, 1)
+    x_reduce(2, 0)
     x_reduce(1, 1)
-    core_reduce(3, 0)
-    core_reduce(3, 1)
 
     pair = four + pool_get(6)
     poolsrc[3] = pair
@@ -393,7 +422,8 @@
     inward = pool_copy(3, 7, at(zl_=(zl + jnp.where(place == 1, 1, 7)) % 8))
     outward = pool_copy(4, 8, at(zl_=(zl + jnp.where(place == 1, 7, 1)) % 8))
     pl.when(middle)(inward.start)
-    x_reduce(2, 0)
+    x_half(3, 1)
+    x_reduce(3, 0)
     x_reduce(2, 1)
 
     @pl.when(middle)
@@ -402,7 +432,6 @@
         poolsrc[4] = poolsrc[3] + poolbuf[7]
         outward.start()
 
-    x_reduce(3, 0)
     x_reduce(3, 1)
 
     @pl.when(jnp.logical_not(middle))
@@ -434,9 +463,9 @@
             ).wait_recv()
         acc[b] = zbuf[b, 0].astype(F32) + zbuf[b, 1].astype(F32)
         if b > 0:
-            over = jnp.logical_and(bit == 1, x >= (2 if b == 1 else 0))
-            if b == 3:
-                over = jnp.logical_or(over, jnp.logical_and(bit == 0, x == 3))
+            over = jnp.logical_and(bit == 1, x < 2)
+            if b > 1:
+                over = jnp.logical_or(over, jnp.logical_and(bit == 0, x >= (3 if b == 2 else 1)))
 
             @pl.when(jnp.logical_and(edge_owner, over))
             def _():
@@ -532,6 +561,7 @@
             pltpu.VMEM((3, 2, 80, 256), BF16),
             pltpu.VMEM((3, 2, 80, 256), BF16),
             pltpu.VMEM((4, 80, 256), F32),
+            pltpu.VMEM((4, 2, 80, 256), F32),
             dma((4,)),
             dma((3,)), dma((3,)),
             dma((6,)), dma((6,)),

time: 67.1 us -> 69 us (1.028)
  Pallas kernels: 65.4 us -> 67.4 us
    pallas_call x1, Pallas kernels: 65.4 us -> 67.4 us  [local(): pl.pallas_call(head_kernel, out_shape=jax.ShapeDtypeStruct((15, 16, 80),...]
where the time goes in v5:
time: 69 us; the launch traced here: 68.8 us
  Pallas kernels  67.4 us (98%)
  local copies, waits for them, and re-layouts  1.46 us (2%)
    pallas_call x1, Pallas kernels, local(): pl.pallas_call(head_kernel, out_shape=jax.ShapeDtypeStruct((15, 16, 80),...  67.4 us
    unnamed x1, local copies, waits for them, and re-layouts  1.46 us

profile of v5, /device:TPU:1, one launch (start us, length us, event | category | flops | bytes accessed | tf_op | source)
XLA Modules:
  0.0 68.8 jit_solution(14704838125662346261)
XLA Ops:
  0.0 67.4 %aspp_head.1 = bf16[15,16,80]{2,1,0:T(8,128)(2,1)} custom-call(bf16[15,80,128]{2,1,0:T(8,128)(2,1)} %bitcast.4, bf16[128,256]{1,0:T(8,128)(2,1)} %pw.1, bf16[3,9,128,256]{3,2,1,0:T(8,128)(2,1)} %bitcast.3, bf16[128,256]{1,0:T(8,128)(2,1)} %wpool.1, bf16[1280,256]{1,0:T(8,128)(2,1)} %wproj.1, f32[6,256]{1,0:T(8,128)} %gain.1, f32[6,256]{1,0:T(8,128)} %shift.1), custom_call_target="tpu_custom_call" | custom-call | tf_op jit(solution)/shard_map/aspp_head/pallas_call | solution.py:538
  67.4 1.5 %copy.9 = bf16[80,15,16]{0,2,1:T(8,128)(2,1)} copy(bf16[80,15,16]{0,2,1:T(8,128)(2,1)} %bitcast.5) | data formatting | bytes 76800

commit v6 on v5

--- a/solution.py
+++ b/solution.py
@@ -13,9 +13,9 @@
 
 
 def head_kernel(
-    feat, pw, wa, wpool, wproj, gain, shift, out,
+    feat, pw, wa, wpool_h, wproj, gain_h, shift_h, out,
     xin, xb, part, cbuf, xbuf, zsrc, zbuf, stage, obuf,
-    pwv, wav, wprojv, poolsrc, poolbuf,
+    pwv, wav, wprojv, wpool, gain, shift, poolsrc, poolbuf,
     part2, cbuf2, xbuf2, zsrc2, zbuf2, acc, xacc,
     ld_sem, ys, yr, hs, hr, cs, cr, xs, xr, zs, zr, os, orr, ps, pr,
     cs2, cr2, xs2, xr2, zs2, zr2,
@@ -43,7 +43,7 @@
 
     bit = ((z + 12) % 16) // 8
     zl_dst = (zl + 4) % 8
-    k = bit * 8 + x * 2 + c
+    k = bit * 8 + c * 4 + x
     kj, kt = k // 3, k % 3
     kq = block_of(kj, zl_dst)
     kg = 4 * kq + y
@@ -51,15 +51,6 @@
     slot = (kg % 5) * 3 + kt
     has_col = k < 15
 
-    loads = [
-        pltpu.make_async_copy(feat, xin, ld_sem.at[0]),
-        pltpu.make_async_copy(pw, pwv, ld_sem.at[1]),
-        pltpu.make_async_copy(wa, wav, ld_sem.at[2]),
-        pltpu.make_async_copy(wproj, wprojv, ld_sem.at[3]),
-    ]
-    for load in loads:
-        load.start()
-
     barrier = pltpu.get_barrier_semaphore()
 
     def hello(dev):
@@ -91,6 +82,16 @@
         hello(at(x_=(x + d) % 4))
     hello(at(c_=1 - c))
 
+    loads = [
+        pltpu.make_async_copy(src, dst, ld_sem.at[i])
+        for i, (src, dst) in enumerate((
+            (feat, xin), (wpool_h, wpool), (pw, pwv), (wa, wav),
+            (wproj, wprojv), (gain_h, gain), (shift_h, shift),
+        ))
+    ]
+    for load in loads:
+        load.start()
+
     zrow = jnp.zeros((3, PAD, 128), BF16)
 
     def clear(i, carry):
@@ -108,10 +109,9 @@
     def _():
         for d in range(3):
             xb[jnp.where(zl == 0, d, 8 + d), :, pl.ds(PAD, 80), :] = blank
-        part2[0, 0, 1, 0] = jnp.zeros((80, 256), BF16)
-        part2[2, 0, 0, 1] = jnp.zeros((80, 256), BF16)
 
     loads[0].wait()
+    loads[1].wait()
     xb[y + 3, :, pl.ds(PAD, 80), :] = xin[0:3]
     xb[y + 4, :, pl.ds(PAD, 80), :] = xin[12:15]
 
@@ -185,8 +185,8 @@
         for side in range(2):
             pl.when(halo_in[side])(halo_copy(d, side).wait_recv)
 
-    loads[1].wait()
     loads[2].wait()
+    loads[3].wait()
 
     def compute(b, lo, hi):
         def body(j, carry):
@@ -208,7 +208,7 @@
             res = res.astype(BF16).reshape(3, 80, 256)
             for t in range(3):
                 s = 3 * j + t
-                part[b, s % 2, s // 8, (s // 2) % 4] = res[t]
+                part[b, (s // 4) % 2, s // 8, s % 4] = res[t]
             return carry
 
         lax.fori_loop(lo, hi, body, 0)
@@ -266,7 +266,10 @@
         )
         z_copies[b, h].start()
 
-    extra = ((3, 0, 1, 4), (3, 1, 0, 2), (2, 0, 3, 4), (2, 1, 0, 2), (1, 1, 0, 2))
+    extra = (
+        (3, 0, 0, 3, 4), (3, 0, 1, 0, 4), (3, 1, 0, 0, 4),
+        (2, 0, 1, 2, 4), (2, 1, 0, 0, 4), (1, 1, 0, 1, 4),
+    )
 
     def within(to, lo, hi):
         return jnp.logical_and(to >= lo, to < hi)
@@ -288,17 +291,22 @@
             res = res.astype(BF16).reshape(3, 80, 256)
             for t in range(3):
                 s = 3 * j + t
-                part2[b - 1, s % 2, s // 8, (s // 2) % 4] = res[t]
+                part2[b - 1, (s // 4) % 2, s // 8, s % 4] = res[t]
             return carry
 
         lax.fori_loop(4 - b, 4, body, 0)
 
-    def extra_core(b, h, lo, hi):
+    def extra_core(b, h, cc, lo, hi):
         n = hi - lo
         return remote(
-            part2.at[b - 1, 1 - c, h, pl.ds(lo, n)], cbuf2.at[b - 1, h, pl.ds(lo, n)],
+            part2.at[b - 1, cc, h, pl.ds(lo, n)], cbuf2.at[b - 1, h, pl.ds(lo, n)],
             cs2.at[b - 1, h], cr2.at[b - 1, h], at(c_=1 - c),
         )
+
+    def extra_core_send(b):
+        for u in extra:
+            if u[0] == b:
+                pl.when(c != u[2])(extra_core(*u).start)
 
     def extra_x(b, h, d):
         to = (x + d) % 4
@@ -314,29 +322,34 @@
             ((zz % 8) * 4 + y, (zz // 8) * 8 + x * 2 + c),
         )
 
-    def extra_core_reduce(b, h, lo, hi):
-        extra_core(b, h, lo, hi).wait_recv()
-        for i in range(lo, hi):
-            mine = part2[b - 1, c, h, i].astype(F32) + cbuf2[b - 1, h, i].astype(F32)
-            part2[b - 1, c, h, i] = mine.astype(BF16)
-        for d in (2, 1, 3):
-            pl.when(within((x + d) % 4, lo, hi))(extra_x(b, h, d).start)
-
-    def extra_x_reduce(b, h, lo, hi):
-        @pl.when(within(x, lo, hi))
+    def extra_core_reduce(b, h, cc, lo, hi):
+        @pl.when(c == cc)
         def _():
-            t = part2[b - 1, c, h, x].astype(F32)
+            extra_core(b, h, cc, lo, hi).wait_recv()
+            for i in range(lo, hi):
+                mine = part2[b - 1, cc, h, i].astype(F32) + cbuf2[b - 1, h, i].astype(F32)
+                part2[b - 1, cc, h, i] = mine.astype(BF16)
+            for d in (2, 1, 3):
+                pl.when(within((x + d) % 4, lo, hi))(extra_x(b, h, d).start)
+
+    def extra_x_reduce(b, h, cc, lo, hi):
+        @pl.when(jnp.logical_and(c == cc, within(x, lo, hi)))
+        def _():
+            t = part2[b - 1, cc, h, x].astype(F32)
             for d in (2, 1, 3):
                 extra_x(b, h, d).wait_recv()
                 t = t + xbuf2[b - 1, h, d - 1].astype(F32)
             zsrc2[b - 1, h] = t.astype(BF16)
             extra_z(b, h).start()
 
-    def extra_sent(b, h, lo, hi):
-        extra_core(b, h, lo, hi).wait_send()
-        for d in (2, 1, 3):
-            pl.when(within((x + d) % 4, lo, hi))(extra_x(b, h, d).wait_send)
-        pl.when(within(x, lo, hi))(extra_z(b, h).wait_send)
+    def extra_sent(b, h, cc, lo, hi):
+        pl.when(c != cc)(extra_core(b, h, cc, lo, hi).wait_send)
+
+        @pl.when(c == cc)
+        def _():
+            for d in (2, 1, 3):
+                pl.when(within((x + d) % 4, lo, hi))(extra_x(b, h, d).wait_send)
+            pl.when(within(x, lo, hi))(extra_z(b, h).wait_send)
 
     compute(0, 0, 3)
     core_send(0, 0)
@@ -353,14 +366,9 @@
 
     @pl.when(edge)
     def _():
-        extra_compute(3)
-        extra_core(*extra[0]).start()
-        extra_core(*extra[1]).start()
-        extra_compute(2)
-        extra_core(*extra[2]).start()
-        extra_core(*extra[3]).start()
-        extra_compute(1)
-        extra_core(*extra[4]).start()
+        for b in (3, 2, 1):
+            extra_compute(b)
+            extra_core_send(b)
 
     core_reduce(1, 0)
     halo_wait(0)
@@ -440,7 +448,8 @@
         poolsrc[4] = poolbuf[8]
 
     pool_send(poolsrc.at[4], 9, at(c_=1 - c))
-    loads[3].wait()
+    for load in loads[4:]:
+        load.wait()
 
     proj = jnp.zeros((80, 256), F32)
     for b in range(4):
@@ -463,9 +472,11 @@
             ).wait_recv()
         acc[b] = zbuf[b, 0].astype(F32) + zbuf[b, 1].astype(F32)
         if b > 0:
-            over = jnp.logical_and(bit == 1, x < 2)
-            if b > 1:
-                over = jnp.logical_or(over, jnp.logical_and(bit == 0, x >= (3 if b == 2 else 1)))
+            over = jnp.zeros((), jnp.bool_)
+            for eb, eh, ec, lo, hi in extra:
+                if eb == b:
+                    mine = jnp.logical_and(bit == eh, c == ec)
+                    over = jnp.logical_or(over, jnp.logical_and(mine, within(x, lo, hi)))
 
             @pl.when(jnp.logical_and(edge_owner, over))
             def _():
@@ -538,7 +549,7 @@
     out = pl.pallas_call(
         head_kernel,
         out_shape=jax.ShapeDtypeStruct((15, 16, 80), BF16),
-        in_specs=[hbm, hbm, hbm, vmem, hbm, vmem, vmem],
+        in_specs=[hbm] * 7,
         out_specs=vmem,
         scratch_shapes=[
             pltpu.VMEM((15, 80, 128), BF16),
@@ -553,6 +564,9 @@
             pltpu.VMEM((128, 256), BF16),
             pltpu.VMEM((3, 9, 128, 256), BF16),
             pltpu.VMEM((1280, 256), BF16),
+            pltpu.VMEM((128, 256), BF16),
+            pltpu.VMEM((6, 256), F32),
+            pltpu.VMEM((6, 256), F32),
             pltpu.VMEM((6, 1, 256), F32),
             pltpu.VMEM((13, 1, 256), F32),
             pltpu.VMEM((3, 2, 2, 4, 80, 256), BF16),
@@ -562,7 +576,7 @@
             pltpu.VMEM((3, 2, 80, 256), BF16),
             pltpu.VMEM((4, 80, 256), F32),
             pltpu.VMEM((4, 2, 80, 256), F32),
-            dma((4,)),
+            dma((7,)),
             dma((3,)), dma((3,)),
             dma((6,)), dma((6,)),
             dma((4, 2)), dma((4, 2)),

time: 69 us -> 65.8 us (0.954)
  Pallas kernels: 67.4 us -> 64.1 us
    pallas_call x1, Pallas kernels: 67.4 us -> 64.1 us  [local(): pl.pallas_call(head_kernel, out_shape=jax.ShapeDtypeStruct((15, 16, 80),...]
where the time goes in v6:
time: 65.8 us; the launch traced here: 65.6 us
  Pallas kernels  64.1 us (97%)
  local copies, waits for them, and re-layouts  1.46 us (2%)
    pallas_call x1, Pallas kernels, local(): pl.pallas_call(head_kernel, out_shape=jax.ShapeDtypeStruct((15, 16, 80),...  64.1 us
    unnamed x1, local copies, waits for them, and re-layouts  1.46 us

profile of v6, /device:TPU:1, one launch (start us, length us, event | category | flops | bytes accessed | tf_op | source)
XLA Modules:
  0.0 65.6 jit_solution(11582087612325387475)
XLA Ops:
  0.0 64.1 %aspp_head.1 = bf16[15,16,80]{2,1,0:T(8,128)(2,1)} custom-call(bf16[15,80,128]{2,1,0:T(8,128)(2,1)} %bitcast.4, bf16[128,256]{1,0:T(8,128)(2,1)} %pw.1, bf16[3,9,128,256]{3,2,1,0:T(8,128)(2,1)} %bitcast.3, bf16[128,256]{1,0:T(8,128)(2,1)} %wpool_h.1, bf16[1280,256]{1,0:T(8,128)(2,1)} %wproj.1, f32[6,256]{1,0:T(8,128)} %gain_h.1, f32[6,256]{1,0:T(8,128)} %shift_h.1), custom_call_target="tpu_custom_call" | custom-call | tf_op jit(solution)/shard_map/aspp_head/pallas_call | solution.py:549
  64.1 1.5 %copy.9 = bf16[80,15,16]{0,2,1:T(8,128)(2,1)} copy(bf16[80,15,16]{0,2,1:T(8,128)(2,1)} %bitcast.5) | data formatting | bytes 76800

commit v7 on v6

--- a/solution.py
+++ b/solution.py
@@ -351,16 +351,25 @@
                 pl.when(within((x + d) % 4, lo, hi))(extra_x(b, h, d).wait_send)
             pl.when(within(x, lo, hi))(extra_z(b, h).wait_send)
 
+    def extra_step(step):
+        @pl.when(edge)
+        def _():
+            for u in extra:
+                step(*u)
+
+    own = poolsrc[0] + pool_get(0) + pool_get(1) + pool_get(2)
+    poolsrc[1] = own
+    pool_send(poolsrc.at[1], 9, at(c_=1 - c))
     compute(0, 0, 3)
     core_send(0, 0)
     compute(0, 3, 5)
     core_send(0, 1)
     compute(1, 0, 3)
     core_send(1, 0)
-    own = poolsrc[0] + pool_get(0) + pool_get(1) + pool_get(2)
-    poolsrc[1] = own
-    pool_send(poolsrc.at[1], 3, at_z(4))
-    pool_send(poolsrc.at[1], 4, at_z(12))
+    both = own + pool_get(9)
+    poolsrc[5] = both
+    for d in range(1, 4):
+        pool_send(poolsrc.at[5], 9 + d, at(x_=(x + d) % 4))
     core_reduce(0, 0)
     core_reduce(0, 1)
 
@@ -371,17 +380,16 @@
             extra_core_send(b)
 
     core_reduce(1, 0)
+    extra_step(extra_core_reduce)
+    here = both + pool_get(10) + pool_get(11) + pool_get(12)
+    poolsrc[2] = here
+    pool_send(poolsrc.at[2], 3, at_z(4))
+    pool_send(poolsrc.at[2], 4, at_z(12))
     halo_wait(0)
     compute(2, 0, 3)
     core_send(2, 0)
     compute(1, 3, 5)
     core_send(1, 1)
-
-    @pl.when(edge)
-    def _():
-        for u in extra:
-            extra_core_reduce(*u)
-
     x_half(0, 0)
     x_half(0, 1)
     core_reduce(2, 0)
@@ -391,76 +399,62 @@
     core_send(3, 0)
     compute(2, 3, 5)
     core_send(2, 1)
-    three = own + pool_get(3) + pool_get(4)
-    pool_send(poolbuf.at[4], 5, at_z(12))
     x_reduce(0, 0)
     x_reduce(0, 1)
     x_half(1, 0)
     core_reduce(3, 0)
     core_reduce(2, 1)
+    three = here + pool_get(3) + pool_get(4)
+    pool_send(poolbuf.at[4], 5, at_z(12))
     halo_wait(2)
     compute(3, 3, 5)
     core_send(3, 1)
+    extra_step(extra_x_reduce)
     x_half(2, 0)
     x_half(1, 1)
     x_reduce(1, 0)
     core_reduce(3, 1)
-    four = three + pool_get(5)
-    poolsrc[2] = four
-    pool_send(poolsrc.at[2], 6, at(zl_=zl + 1 - 2 * (zl % 2)))
-
-    @pl.when(edge)
-    def _():
-        for u in extra:
-            extra_x_reduce(*u)
-
     x_half(3, 0)
     x_half(2, 1)
+    four = three + pool_get(5)
+    poolsrc[3] = four
+    pool_send(poolsrc.at[3], 6, at(zl_=zl + 1 - 2 * (zl % 2)))
     x_reduce(2, 0)
     x_reduce(1, 1)
 
-    pair = four + pool_get(6)
-    poolsrc[3] = pair
     place = zl % 4
     middle = jnp.logical_or(place == 1, place == 2)
 
     def pool_copy(src, slot_i, dev):
         return remote(poolsrc.at[src], poolbuf.at[slot_i], ps.at[slot_i], pr.at[slot_i], dev)
 
-    inward = pool_copy(3, 7, at(zl_=(zl + jnp.where(place == 1, 1, 7)) % 8))
+    inward = pool_copy(6, 7, at(zl_=(zl + jnp.where(place == 1, 1, 7)) % 8))
     outward = pool_copy(4, 8, at(zl_=(zl + jnp.where(place == 1, 7, 1)) % 8))
-    pl.when(middle)(inward.start)
     x_half(3, 1)
     x_reduce(3, 0)
+    poolsrc[6] = four + pool_get(6)
+    pl.when(middle)(inward.start)
     x_reduce(2, 1)
+    x_reduce(3, 1)
 
     @pl.when(middle)
     def _():
         inward.wait_recv()
-        poolsrc[4] = poolsrc[3] + poolbuf[7]
+        poolsrc[4] = poolsrc[6] + poolbuf[7]
         outward.start()
 
-    x_reduce(3, 1)
-
-    @pl.when(jnp.logical_not(middle))
-    def _():
-        outward.wait_recv()
-        poolsrc[4] = poolbuf[8]
-
-    pool_send(poolsrc.at[4], 9, at(c_=1 - c))
     for load in loads[4:]:
         load.wait()
 
     proj = jnp.zeros((80, 256), F32)
     for b in range(4):
-        if b == 1:
-            both = poolsrc[4] + pool_get(9)
-            poolsrc[5] = both
-            for d in range(1, 4):
-                pool_send(poolsrc.at[5], 9 + d, at(x_=(x + d) % 4))
         if b == 3:
-            pre_all = both + pool_get(10) + pool_get(11) + pool_get(12)
-            pre_all = pre_all * (1.0 / 38400.0)
+            @pl.when(jnp.logical_not(middle))
+            def _():
+                outward.wait_recv()
+                poolsrc[4] = poolbuf[8]
+
+            pre_all = poolsrc[4] * (1.0 / 38400.0)
             pooled = jnp.maximum(gain[4:5] * pre_all + shift[4:5], 0.0).astype(BF16)
             pool_term = jnp.dot(
                 jnp.broadcast_to(pooled, (16, 256)), wprojv[pl.ds(1024, 256), :],
@@ -548,7 +542,7 @@
     dma = pltpu.SemaphoreType.DMA
     out = pl.pallas_call(
         head_kernel,
-        out_shape=jax.ShapeDtypeStruct((15, 16, 80), BF16),
+        out_shape=pltpu.VMEM((15, 16, 80), BF16),
         in_specs=[hbm] * 7,
         out_specs=vmem,
         scratch_shapes=[
@@ -567,7 +561,7 @@
             pltpu.VMEM((128, 256), BF16),
             pltpu.VMEM((6, 256), F32),
             pltpu.VMEM((6, 256), F32),
-            pltpu.VMEM((6, 1, 256), F32),
+            pltpu.VMEM((7, 1, 256), F32),
             pltpu.VMEM((13, 1, 256), F32),
             pltpu.VMEM((3, 2, 2, 4, 80, 256), BF16),
             pltpu.VMEM((3, 2, 4, 80, 256), BF16),

time: 65.8 us -> 62.8 us (0.954)
  Pallas kernels: 64.1 us -> 62 us
  local copies, waits for them, and re-layouts: 1.46 us -> 0.63 us
    pallas_call x1, Pallas kernels: 64.1 us -> 62 us  [local(): pl.pallas_call(head_kernel, out_shape=pltpu.VMEM((15, 16, 80), BF16), in_...]
    unnamed x1, local copies, waits for them, and re-layouts: 1.46 us -> 0.63 us
where the time goes in v7:
time: 62.8 us; the launch traced here: 62.6 us
  Pallas kernels  62 us (99%)
  local copies, waits for them, and re-layouts  0.63 us (1%)
    pallas_call x1, Pallas kernels, local(): pl.pallas_call(head_kernel, out_shape=pltpu.VMEM((15, 16, 80), BF16), in_...  62 us

profile of v7, /device:TPU:1, one launch (start us, length us, event | category | flops | bytes accessed | tf_op | source)
XLA Modules:
  0.0 62.6 jit_solution(2608740288173062993)
XLA Ops:
  0.0 62.0 %aspp_head.1 = bf16[15,16,80]{2,1,0:T(8,128)(2,1)S(1)} custom-call(bf16[15,80,128]{2,1,0:T(8,128)(2,1)} %bitcast.5, bf16[128,256]{1,0:T(8,128)(2,1)} %pw.1, bf16[3,9,128,256]{3,2,1,0:T(8,128)(2,1)} %bitcast.4, bf16[128,256]{1,0:T(8,128)(2,1)} %wpool_h.1, bf16[1280,256]{1,0:T(8,128)(2,1)} %wproj.1, f32[6,256]{1,0:T(8,128)} %gain_h.1, f32[6,256]{1,0:T(8,128)} %shift_h.1), custom_call_target="tpu_custom_call" | custom-call | tf_op jit(solution)/shard_map/aspp_head/pallas_call | solution.py:543
  62.0 0.6 %copy.9 = bf16[80,15,16]{0,2,1:T(8,128)(2,1)} copy(bf16[80,15,16]{0,2,1:T(8,128)(2,1)S(1)} %bitcast.3) | data formatting | bytes 76800

commit v8 on v7

--- a/solution.py
+++ b/solution.py
@@ -18,7 +18,7 @@
     pwv, wav, wprojv, wpool, gain, shift, poolsrc, poolbuf,
     part2, cbuf2, xbuf2, zsrc2, zbuf2, acc, xacc,
     ld_sem, ys, yr, hs, hr, cs, cr, xs, xr, zs, zr, os, orr, ps, pr,
-    cs2, cr2, xs2, xr2, zs2, zr2,
+    cs2, cr2, xs2, xr2, zs2, zr2, reach,
 ):
     lon = lax.axis_index("lon")
     ch = lax.axis_index("ch")
@@ -60,23 +60,8 @@
     edge = jnp.logical_or(zl == 0, zl == 7)
     edge_owner = jnp.logical_or(zl == 3, zl == 4)
 
-    @pl.when(edge_owner)
-    def _():
-        far = jnp.where(zl == 4, 7, 0) * 4 + y
-        hello((far, x * 2 + c))
-        hello((far, 8 + x * 2 + c))
-
-    @pl.when(zl < 7)
-    def _():
-        hello(east)
-
-    @pl.when(zl > 0)
-    def _():
-        hello(west)
-
-    hello(at_z(4))
-    hello(at_z(12))
-
+    hello(at_z(1))
+    hello(at_z(15))
     for d in range(1, 4):
         hello(at(y_=(y + d) % 4))
         hello(at(x_=(x + d) % 4))
@@ -92,6 +77,74 @@
     for load in loads:
         load.start()
 
+    pl.semaphore_wait(barrier, 9)
+
+    def remote(src, dst, ssem, rsem, dev):
+        return pltpu.make_async_remote_copy(
+            src_ref=src, dst_ref=dst, send_sem=ssem, recv_sem=rsem,
+            device_id=dev, device_id_type=MESH_ID,
+        )
+
+    def reach_signal(r):
+        for dz in (1, 15):
+            pl.semaphore_signal(
+                reach.at[r], inc=1, device_id=at_z(dz), device_id_type=MESH_ID
+            )
+
+    def reach_wait(r):
+        pl.semaphore_wait(reach.at[r], 2)
+
+    rows = pl.ds(PAD, 80)
+    ycopies = []
+    for g in range(1, 4):
+        q = (5 * y + g) // 4
+        copy = remote(
+            feat.at[pl.ds(3 * g, 3)], xb.at[q + 3, :, rows, :],
+            ys.at[g - 1], yr.at[g - 1], at(y_=(y + g) % 4),
+        )
+        copy.start()
+        ycopies.append(copy)
+    psends = {}
+
+    def pool_send(src, slot_i, dev):
+        psends[slot_i] = remote(src, poolbuf.at[slot_i], ps.at[slot_i], pr.at[slot_i], dev)
+        psends[slot_i].start()
+
+    def pool_get(slot_i):
+        psends[slot_i].wait_recv()
+        return poolbuf[slot_i]
+
+    loads[0].wait()
+    xb[y + 3, :, rows, :] = xin[0:3]
+    xb[y + 4, :, rows, :] = xin[12:15]
+    reach_signal(0)
+
+    def halo_copy(d, side):
+        q = (4 - d) if side == 0 else d
+        q_to = q - 5 if side == 0 else q + 5
+        return remote(
+            xb.at[q + 3, :, rows, :], xb.at[q_to + 3, :, rows, :],
+            hs.at[2 * d + side], hr.at[2 * d + side], east if side == 0 else west,
+        )
+
+    halo_out = (zl < 7, zl > 0)
+    halo_in = (zl > 0, zl < 7)
+    for d, sides in ((0, (0,)), (0, (1,)), (1, (0,)), (1, (1,)), (2, (0, 1))):
+        q = (4 - d) if sides[0] == 0 else d
+        g = (4 * q + y) % 5
+
+        @pl.when(jnp.logical_and(g > 0, g < 4))
+        def _():
+            gi = jnp.clip(g - 1, 0, 2)
+            remote(
+                xin.at[pl.ds(0, 3)], xb.at[q + 3, :, rows, :], ys.at[gi], yr.at[gi], east
+            ).wait_recv()
+
+        for side in sides:
+            pl.when(halo_out[side])(halo_copy(d, side).start)
+
+    reach_wait(0)
+    reach_signal(1)
     zrow = jnp.zeros((3, PAD, 128), BF16)
 
     def clear(i, carry):
@@ -110,10 +163,7 @@
         for d in range(3):
             xb[jnp.where(zl == 0, d, 8 + d), :, pl.ds(PAD, 80), :] = blank
 
-    loads[0].wait()
     loads[1].wait()
-    xb[y + 3, :, pl.ds(PAD, 80), :] = xin[0:3]
-    xb[y + 4, :, pl.ds(PAD, 80), :] = xin[12:15]
 
     def add_col(i, tot):
         return tot + jnp.sum(xin[i].astype(F32).reshape(10, 8, 128), axis=0)
@@ -126,60 +176,8 @@
     )[0:1]
     poolsrc[0] = pre
 
-    pl.semaphore_wait(barrier, 11 + edge.astype(jnp.int32))
-
-    def remote(src, dst, ssem, rsem, dev):
-        return pltpu.make_async_remote_copy(
-            src_ref=src, dst_ref=dst, send_sem=ssem, recv_sem=rsem,
-            device_id=dev, device_id_type=MESH_ID,
-        )
-
-    rows = pl.ds(PAD, 80)
-    ycopies = []
-    for g in range(1, 4):
-        q = (5 * y + g) // 4
-        copy = remote(
-            xin.at[pl.ds(3 * g, 3)], xb.at[q + 3, :, rows, :],
-            ys.at[g - 1], yr.at[g - 1], at(y_=(y + g) % 4),
-        )
-        copy.start()
-        ycopies.append(copy)
-    psends = {}
-
-    def pool_send(src, slot_i, dev):
-        psends[slot_i] = remote(src, poolbuf.at[slot_i], ps.at[slot_i], pr.at[slot_i], dev)
-        psends[slot_i].start()
-
-    def pool_get(slot_i):
-        psends[slot_i].wait_recv()
-        return poolbuf[slot_i]
-
     for d in range(1, 4):
         pool_send(poolsrc.at[0], d - 1, at(y_=(y + d) % 4))
-
-    def halo_copy(d, side):
-        q = (4 - d) if side == 0 else d
-        q_to = q - 5 if side == 0 else q + 5
-        return remote(
-            xb.at[q + 3, :, rows, :], xb.at[q_to + 3, :, rows, :],
-            hs.at[2 * d + side], hr.at[2 * d + side], east if side == 0 else west,
-        )
-
-    halo_out = (zl < 7, zl > 0)
-    halo_in = (zl > 0, zl < 7)
-    for d, sides in ((0, (0,)), (0, (1,)), (1, (0,)), (1, (1,)), (2, (0, 1))):
-        q = (4 - d) if sides[0] == 0 else d
-        g = (4 * q + y) % 5
-
-        @pl.when(jnp.logical_and(g > 0, g < 4))
-        def _():
-            gi = jnp.clip(g - 1, 0, 2)
-            remote(
-                xin.at[pl.ds(0, 3)], xb.at[q + 3, :, rows, :], ys.at[gi], yr.at[gi], east
-            ).wait_recv()
-
-        for side in sides:
-            pl.when(halo_out[side])(halo_copy(d, side).start)
 
     def halo_wait(d):
         for side in range(2):
@@ -357,21 +355,23 @@
             for u in extra:
                 step(*u)
 
-    own = poolsrc[0] + pool_get(0) + pool_get(1) + pool_get(2)
-    poolsrc[1] = own
-    pool_send(poolsrc.at[1], 9, at(c_=1 - c))
     compute(0, 0, 3)
     core_send(0, 0)
     compute(0, 3, 5)
     core_send(0, 1)
+    own = poolsrc[0] + pool_get(0) + pool_get(1) + pool_get(2)
+    poolsrc[1] = own
+    pool_send(poolsrc.at[1], 9, at(c_=1 - c))
+    reach_wait(1)
+    reach_signal(2)
     compute(1, 0, 3)
     core_send(1, 0)
+    core_reduce(0, 0)
+    core_reduce(0, 1)
     both = own + pool_get(9)
     poolsrc[5] = both
     for d in range(1, 4):
         pool_send(poolsrc.at[5], 9 + d, at(x_=(x + d) % 4))
-    core_reduce(0, 0)
-    core_reduce(0, 1)
 
     @pl.when(edge)
     def _():
@@ -379,19 +379,25 @@
             extra_compute(b)
             extra_core_send(b)
 
+    reach_wait(2)
+    reach_signal(3)
     core_reduce(1, 0)
     extra_step(extra_core_reduce)
-    here = both + pool_get(10) + pool_get(11) + pool_get(12)
-    poolsrc[2] = here
-    pool_send(poolsrc.at[2], 3, at_z(4))
-    pool_send(poolsrc.at[2], 4, at_z(12))
+    x_half(0, 0)
+    x_half(0, 1)
     halo_wait(0)
     compute(2, 0, 3)
     core_send(2, 0)
     compute(1, 3, 5)
     core_send(1, 1)
-    x_half(0, 0)
-    x_half(0, 1)
+    reach_wait(3)
+    here = both + pool_get(10) + pool_get(11) + pool_get(12)
+    poolsrc[2] = here
+    pool_send(poolsrc.at[2], 3, at_z(4))
+    pool_send(poolsrc.at[2], 4, at_z(12))
+    x_half(1, 0)
+    x_reduce(0, 0)
+    x_reduce(0, 1)
     core_reduce(2, 0)
     core_reduce(1, 1)
     halo_wait(1)
@@ -399,28 +405,25 @@
     core_send(3, 0)
     compute(2, 3, 5)
     core_send(2, 1)
-    x_reduce(0, 0)
-    x_reduce(0, 1)
-    x_half(1, 0)
+    x_reduce(1, 0)
+    extra_step(extra_x_reduce)
+    x_half(2, 0)
+    x_half(1, 1)
     core_reduce(3, 0)
     core_reduce(2, 1)
-    three = here + pool_get(3) + pool_get(4)
-    pool_send(poolbuf.at[4], 5, at_z(12))
     halo_wait(2)
     compute(3, 3, 5)
     core_send(3, 1)
-    extra_step(extra_x_reduce)
-    x_half(2, 0)
-    x_half(1, 1)
-    x_reduce(1, 0)
-    core_reduce(3, 1)
+    three = here + pool_get(3) + pool_get(4)
+    pool_send(poolbuf.at[4], 5, at_z(12))
+    x_reduce(2, 0)
+    x_reduce(1, 1)
     x_half(3, 0)
     x_half(2, 1)
+    core_reduce(3, 1)
     four = three + pool_get(5)
     poolsrc[3] = four
     pool_send(poolsrc.at[3], 6, at(zl_=zl + 1 - 2 * (zl % 2)))
-    x_reduce(2, 0)
-    x_reduce(1, 1)
 
     place = zl % 4
     middle = jnp.logical_or(place == 1, place == 2)
@@ -430,11 +433,11 @@
 
     inward = pool_copy(6, 7, at(zl_=(zl + jnp.where(place == 1, 1, 7)) % 8))
     outward = pool_copy(4, 8, at(zl_=(zl + jnp.where(place == 1, 7, 1)) % 8))
+    x_reduce(3, 0)
     x_half(3, 1)
-    x_reduce(3, 0)
+    x_reduce(2, 1)
     poolsrc[6] = four + pool_get(6)
     pl.when(middle)(inward.start)
-    x_reduce(2, 1)
     x_reduce(3, 1)
 
     @pl.when(middle)
@@ -581,6 +584,7 @@
             dma((3, 2)), dma((3, 2)),
             dma((3, 2, 3)), dma((3, 2, 3)),
             dma((3, 2)), dma((3, 2)),
+            pltpu.SemaphoreType.REGULAR((4,)),
         ],
         compiler_params=pltpu.CompilerParams(collective_id=0, has_side_effects=True),
         name="aspp_head",

time: 62.8 us -> 66.9 us (1.065)
  Pallas kernels: 62 us -> 66.2 us
    pallas_call x1, Pallas kernels: 62 us -> 66.2 us  [local(): pl.pallas_call(head_kernel, out_shape=pltpu.VMEM((15, 16, 80), BF16), in_...]
where the time goes in v8:
time: 66.9 us; the launch traced here: 66.8 us
  Pallas kernels  66.2 us (99%)
    pallas_call x1, Pallas kernels, local(): pl.pallas_call(head_kernel, out_shape=pltpu.VMEM((15, 16, 80), BF16), in_...  66.2 us

profile of v8, /device:TPU:1, one launch (start us, length us, event | category | flops | bytes accessed | tf_op | source)
XLA Modules:
  0.0 66.8 jit_solution(10538042333416432627)
XLA Ops:
  0.0 66.2 %aspp_head.1 = bf16[15,16,80]{2,1,0:T(8,128)(2,1)S(1)} custom-call(bf16[15,80,128]{2,1,0:T(8,128)(2,1)} %bitcast.5, bf16[128,256]{1,0:T(8,128)(2,1)} %pw.1, bf16[3,9,128,256]{3,2,1,0:T(8,128)(2,1)} %bitcast.4, bf16[128,256]{1,0:T(8,128)(2,1)} %wpool_h.1, bf16[1280,256]{1,0:T(8,128)(2,1)} %wproj.1, f32[6,256]{1,0:T(8,128)} %gain_h.1, f32[6,256]{1,0:T(8,128)} %shift_h.1), custom_call_target="tpu_custom_call" | custom-call | tf_op jit(solution)/shard_map/aspp_head/pallas_call | solution.py:546
  66.2 0.6 copy.9

commit v9 on v8

--- a/solution.py
+++ b/solution.py
@@ -366,12 +366,12 @@
     reach_signal(2)
     compute(1, 0, 3)
     core_send(1, 0)
-    core_reduce(0, 0)
-    core_reduce(0, 1)
     both = own + pool_get(9)
     poolsrc[5] = both
     for d in range(1, 4):
         pool_send(poolsrc.at[5], 9 + d, at(x_=(x + d) % 4))
+    core_reduce(0, 0)
+    core_reduce(0, 1)
 
     @pl.when(edge)
     def _():
@@ -379,12 +379,10 @@
             extra_compute(b)
             extra_core_send(b)
 
+    core_reduce(1, 0)
     reach_wait(2)
     reach_signal(3)
-    core_reduce(1, 0)
     extra_step(extra_core_reduce)
-    x_half(0, 0)
-    x_half(0, 1)
     halo_wait(0)
     compute(2, 0, 3)
     core_send(2, 0)
@@ -395,9 +393,8 @@
     poolsrc[2] = here
     pool_send(poolsrc.at[2], 3, at_z(4))
     pool_send(poolsrc.at[2], 4, at_z(12))
-    x_half(1, 0)
-    x_reduce(0, 0)
-    x_reduce(0, 1)
+    x_half(0, 0)
+    x_half(0, 1)
     core_reduce(2, 0)
     core_reduce(1, 1)
     halo_wait(1)
@@ -405,25 +402,28 @@
     core_send(3, 0)
     compute(2, 3, 5)
     core_send(2, 1)
-    x_reduce(1, 0)
+    x_reduce(0, 0)
+    x_reduce(0, 1)
+    x_half(1, 0)
+    core_reduce(3, 0)
+    core_reduce(2, 1)
+    three = here + pool_get(3) + pool_get(4)
+    pool_send(poolbuf.at[4], 5, at_z(12))
+    halo_wait(2)
+    compute(3, 3, 5)
+    core_send(3, 1)
     extra_step(extra_x_reduce)
     x_half(2, 0)
     x_half(1, 1)
-    core_reduce(3, 0)
-    core_reduce(2, 1)
-    halo_wait(2)
-    compute(3, 3, 5)
-    core_send(3, 1)
-    three = here + pool_get(3) + pool_get(4)
-    pool_send(poolbuf.at[4], 5, at_z(12))
-    x_reduce(2, 0)
-    x_reduce(1, 1)
+    x_reduce(1, 0)
+    core_reduce(3, 1)
     x_half(3, 0)
     x_half(2, 1)
-    core_reduce(3, 1)
     four = three + pool_get(5)
     poolsrc[3] = four
     pool_send(poolsrc.at[3], 6, at(zl_=zl + 1 - 2 * (zl % 2)))
+    x_reduce(2, 0)
+    x_reduce(1, 1)
 
     place = zl % 4
     middle = jnp.logical_or(place == 1, place == 2)
@@ -433,11 +433,11 @@
 
     inward = pool_copy(6, 7, at(zl_=(zl + jnp.where(place == 1, 1, 7)) % 8))
     outward = pool_copy(4, 8, at(zl_=(zl + jnp.where(place == 1, 7, 1)) % 8))
+    x_half(3, 1)
     x_reduce(3, 0)
-    x_half(3, 1)
-    x_reduce(2, 1)
     poolsrc[6] = four + pool_get(6)
     pl.when(middle)(inward.start)
+    x_reduce(2, 1)
     x_reduce(3, 1)
 
     @pl.when(middle)

time: 66.9 us -> 64.8 us (0.969)
  Pallas kernels: 66.2 us -> 64 us
    pallas_call x1, Pallas kernels: 66.2 us -> 64 us  [local(): pl.pallas_call(head_kernel, out_shape=pltpu.VMEM((15, 16, 80), BF16), in_...]
where the time goes in v9:
time: 64.8 us; the launch traced here: 64.7 us
  Pallas kernels  64 us (99%)
    pallas_call x1, Pallas kernels, local(): pl.pallas_call(head_kernel, out_shape=pltpu.VMEM((15, 16, 80), BF16), in_...  64 us

profile of v9, /device:TPU:1, one launch (start us, length us, event | category | flops | bytes accessed | tf_op | source)
XLA Modules:
  0.0 64.7 jit_solution(1983199777945247207)
XLA Ops:
  0.0 64.0 %aspp_head.1 = bf16[15,16,80]{2,1,0:T(8,128)(2,1)S(1)} custom-call(bf16[15,80,128]{2,1,0:T(8,128)(2,1)} %bitcast.5, bf16[128,256]{1,0:T(8,128)(2,1)} %pw.1, bf16[3,9,128,256]{3,2,1,0:T(8,128)(2,1)} %bitcast.4, bf16[128,256]{1,0:T(8,128)(2,1)} %wpool_h.1, bf16[1280,256]{1,0:T(8,128)(2,1)} %wproj.1, f32[6,256]{1,0:T(8,128)} %gain_h.1, f32[6,256]{1,0:T(8,128)} %shift_h.1), custom_call_target="tpu_custom_call" | custom-call | tf_op jit(solution)/shard_map/aspp_head/pallas_call | solution.py:546
  64.0 0.6 copy.9

commit v10 on v7

--- a/solution.py
+++ b/solution.py
@@ -92,6 +92,37 @@
     for load in loads:
         load.start()
 
+    pl.semaphore_wait(barrier, 11 + edge.astype(jnp.int32))
+
+    def remote(src, dst, ssem, rsem, dev):
+        return pltpu.make_async_remote_copy(
+            src_ref=src, dst_ref=dst, send_sem=ssem, recv_sem=rsem,
+            device_id=dev, device_id_type=MESH_ID,
+        )
+
+    rows = pl.ds(PAD, 80)
+    ycopies = []
+    for g in range(1, 4):
+        q = (5 * y + g) // 4
+        copy = remote(
+            feat.at[pl.ds(3 * g, 3)], xb.at[q + 3, :, rows, :],
+            ys.at[g - 1], yr.at[g - 1], at(y_=(y + g) % 4),
+        )
+        copy.start()
+        ycopies.append(copy)
+    psends = {}
+
+    def pool_send(src, slot_i, dev):
+        psends[slot_i] = remote(src, poolbuf.at[slot_i], ps.at[slot_i], pr.at[slot_i], dev)
+        psends[slot_i].start()
+
+    def pool_get(slot_i):
+        psends[slot_i].wait_recv()
+        return poolbuf[slot_i]
+
+    loads[0].wait()
+    xb[y + 3, :, rows, :] = xin[0:3]
+    xb[y + 4, :, rows, :] = xin[12:15]
     zrow = jnp.zeros((3, PAD, 128), BF16)
 
     def clear(i, carry):
@@ -110,10 +141,7 @@
         for d in range(3):
             xb[jnp.where(zl == 0, d, 8 + d), :, pl.ds(PAD, 80), :] = blank
 
-    loads[0].wait()
     loads[1].wait()
-    xb[y + 3, :, pl.ds(PAD, 80), :] = xin[0:3]
-    xb[y + 4, :, pl.ds(PAD, 80), :] = xin[12:15]
 
     def add_col(i, tot):
         return tot + jnp.sum(xin[i].astype(F32).reshape(10, 8, 128), axis=0)
@@ -125,34 +153,6 @@
         precision=lax.Precision.HIGHEST, preferred_element_type=F32,
     )[0:1]
     poolsrc[0] = pre
-
-    pl.semaphore_wait(barrier, 11 + edge.astype(jnp.int32))
-
-    def remote(src, dst, ssem, rsem, dev):
-        return pltpu.make_async_remote_copy(
-            src_ref=src, dst_ref=dst, send_sem=ssem, recv_sem=rsem,
-            device_id=dev, device_id_type=MESH_ID,
-        )
-
-    rows = pl.ds(PAD, 80)
-    ycopies = []
-    for g in range(1, 4):
-        q = (5 * y + g) // 4
-        copy = remote(
-            xin.at[pl.ds(3 * g, 3)], xb.at[q + 3, :, rows, :],
-            ys.at[g - 1], yr.at[g - 1], at(y_=(y + g) % 4),
-        )
-        copy.start()
-        ycopies.append(copy)
-    psends = {}
-
-    def pool_send(src, slot_i, dev):
-        psends[slot_i] = remote(src, poolbuf.at[slot_i], ps.at[slot_i], pr.at[slot_i], dev)
-        psends[slot_i].start()
-
-    def pool_get(slot_i):
-        psends[slot_i].wait_recv()
-        return poolbuf[slot_i]
 
     for d in range(1, 4):
         pool_send(poolsrc.at[0], d - 1, at(y_=(y + d) % 4))

time: 62.8 us -> 63.2 us (level)
  no operation moved by 1% of the time
where the time goes in v10:
time: 63.2 us; the launch traced here: 63.1 us
  Pallas kernels  62.4 us (99%)
    pallas_call x1, Pallas kernels, local(): pl.pallas_call(head_kernel, out_shape=pltpu.VMEM((15, 16, 80), BF16), in_...  62.4 us

profile of v10, /device:TPU:1, one launch (start us, length us, event | category | flops | bytes accessed | tf_op | source)
XLA Modules:
  0.0 63.1 jit_solution(11120997619625822324)
XLA Ops:
  0.0 62.4 %aspp_head.1 = bf16[15,16,80]{2,1,0:T(8,128)(2,1)S(1)} custom-call(bf16[15,80,128]{2,1,0:T(8,128)(2,1)} %bitcast.5, bf16[128,256]{1,0:T(8,128)(2,1)} %pw.1, bf16[3,9,128,256]{3,2,1,0:T(8,128)(2,1)} %bitcast.4, bf16[128,256]{1,0:T(8,128)(2,1)} %wpool_h.1, bf16[1280,256]{1,0:T(8,128)(2,1)} %wproj.1, f32[6,256]{1,0:T(8,128)} %gain_h.1, f32[6,256]{1,0:T(8,128)} %shift_h.1), custom_call_target="tpu_custom_call" | custom-call | tf_op jit(solution)/shard_map/aspp_head/pallas_call | solution.py:543
  62.5 0.6 copy.9

commit v11 on v7

--- a/solution.py
+++ b/solution.py
@@ -231,8 +231,18 @@
             return carry
 
         lax.fori_loop(0, 4, body, 0)
+        x_copies[b, h] = []
+        if (b, h) in direct:
+            for d in (2, 1, 3):
+                to = (x + d) % 4
+                copy = remote(
+                    part.at[b, c, h, to], xbuf.at[b, h, d - 1],
+                    xs.at[b, h, d - 1], xr.at[b, h, d - 1], at(x_=to),
+                )
+                copy.start()
+                x_copies[b, h].append(copy)
+            return
         first = flip if h == 0 else 3 - x
-        x_copies[b, h] = []
         for i, col in enumerate((first, (x + 2) % 4)):
             copy = remote(
                 part.at[b, c, h, col], xbuf.at[b, h, i], xs.at[b, h, i], xr.at[b, h, i],
@@ -242,6 +252,7 @@
             x_copies[b, h].append(copy)
 
     flip = x + 1 - 2 * (x % 2)
+    direct = ((3, 1),)
 
     def x_half(b, h):
         second = 3 - x if h == 0 else flip
@@ -258,8 +269,15 @@
         xacc[b, h] = part[b, c, h, x].astype(F32) + xbuf[b, h, 0].astype(F32)
 
     def x_reduce(b, h):
-        x_copies[b, h][2].wait_recv()
-        zsrc[b, h] = (xacc[b, h] + xbuf[b, h, 2].astype(F32)).astype(BF16)
+        if (b, h) in direct:
+            total = part[b, c, h, x].astype(F32)
+            for i, copy in enumerate(x_copies[b, h]):
+                copy.wait_recv()
+                total = total + xbuf[b, h, (1, 0, 2)[i]].astype(F32)
+            zsrc[b, h] = total.astype(BF16)
+        else:
+            x_copies[b, h][2].wait_recv()
+            zsrc[b, h] = (xacc[b, h] + xbuf[b, h, 2].astype(F32)).astype(BF16)
         up = (zh == h).astype(jnp.int32)
         z_copies[b, h] = remote(
             zsrc.at[b, h], zbuf.at[b, 1 - up], zs.at[b, h], zr.at[b, 1 - up], at_z(12 - 8 * up)
@@ -410,10 +428,10 @@
     compute(3, 3, 5)
     core_send(3, 1)
     extra_step(extra_x_reduce)
+    core_reduce(3, 1)
     x_half(2, 0)
     x_half(1, 1)
     x_reduce(1, 0)
-    core_reduce(3, 1)
     x_half(3, 0)
     x_half(2, 1)
     four = three + pool_get(5)
@@ -430,7 +448,6 @@
 
     inward = pool_copy(6, 7, at(zl_=(zl + jnp.where(place == 1, 1, 7)) % 8))
     outward = pool_copy(4, 8, at(zl_=(zl + jnp.where(place == 1, 7, 1)) % 8))
-    x_half(3, 1)
     x_reduce(3, 0)
     poolsrc[6] = four + pool_get(6)
     pl.when(middle)(inward.start)

time: 62.8 us -> 64 us (1.019)
  Pallas kernels: 62 us -> 63.2 us
    pallas_call x1, Pallas kernels: 62 us -> 63.2 us  [local(): pl.pallas_call(head_kernel, out_shape=pltpu.VMEM((15, 16, 80), BF16), in_...]
where the time goes in v11:
time: 64 us; the launch traced here: 63.8 us
  Pallas kernels  63.2 us (99%)
    pallas_call x1, Pallas kernels, local(): pl.pallas_call(head_kernel, out_shape=pltpu.VMEM((15, 16, 80), BF16), in_...  63.2 us

profile of v11, /device:TPU:1, one launch (start us, length us, event | category | flops | bytes accessed | tf_op | source)
XLA Modules:
  0.0 63.8 jit_solution(15480565506807940028)
XLA Ops:
  0.0 63.2 %aspp_head.1 = bf16[15,16,80]{2,1,0:T(8,128)(2,1)S(1)} custom-call(bf16[15,80,128]{2,1,0:T(8,128)(2,1)} %bitcast.5, bf16[128,256]{1,0:T(8,128)(2,1)} %pw.1, bf16[3,9,128,256]{3,2,1,0:T(8,128)(2,1)} %bitcast.4, bf16[128,256]{1,0:T(8,128)(2,1)} %wpool_h.1, bf16[1280,256]{1,0:T(8,128)(2,1)} %wproj.1, f32[6,256]{1,0:T(8,128)} %gain_h.1, f32[6,256]{1,0:T(8,128)} %shift_h.1), custom_call_target="tpu_custom_call" | custom-call | tf_op jit(solution)/shard_map/aspp_head/pallas_call | solution.py:560
  63.2 0.6 copy.9

commit v12 on v7

--- a/solution.py
+++ b/solution.py
@@ -490,14 +490,13 @@
     def out_copy(d):
         return remote(stage.at[d], obuf.at[slot], os.at[d], orr.at[slot], (zl_dst * 4 + y_dst, d))
 
-    def out_send(i, carry):
-        @pl.when(has_col)
-        def _():
-            out_copy((ch + i) % 16).start()
-
-        return carry
-
-    lax.fori_loop(0, 16, out_send, 0)
+    @pl.when(has_col)
+    def _():
+        for dx in (2, 1, 3, 0):
+            for cc in range(2):
+                for half in range(2):
+                    out_copy(half * 8 + (x + dx) % 4 * 2 + cc).start()
+
     for copy in ycopies + list(psends.values()):
         copy.wait_send()
     for d in range(3):

time: 62.8 us -> 62.6 us (level)
  no operation moved by 1% of the time
where the time goes in v12:
time: 62.6 us; the launch traced here: 62.4 us
  Pallas kernels  61.8 us (99%)
  local copies, waits for them, and re-layouts  0.63 us (1%)
    pallas_call x1, Pallas kernels, local(): pl.pallas_call(head_kernel, out_shape=pltpu.VMEM((15, 16, 80), BF16), in_...  61.8 us

profile of v12, /device:TPU:1, one launch (start us, length us, event | category | flops | bytes accessed | tf_op | source)
XLA Modules:
  0.0 62.4 jit_solution(1969302502563443624)
XLA Ops:
  0.0 61.8 %aspp_head.1 = bf16[15,16,80]{2,1,0:T(8,128)(2,1)S(1)} custom-call(bf16[15,80,128]{2,1,0:T(8,128)(2,1)} %bitcast.5, bf16[128,256]{1,0:T(8,128)(2,1)} %pw.1, bf16[3,9,128,256]{3,2,1,0:T(8,128)(2,1)} %bitcast.4, bf16[128,256]{1,0:T(8,128)(2,1)} %wpool_h.1, bf16[1280,256]{1,0:T(8,128)(2,1)} %wproj.1, f32[6,256]{1,0:T(8,128)} %gain_h.1, f32[6,256]{1,0:T(8,128)} %shift_h.1), custom_call_target="tpu_custom_call" | custom-call | tf_op jit(solution)/shard_map/aspp_head/pallas_call | solution.py:542
  61.8 0.6 %copy.9 = bf16[80,15,16]{0,2,1:T(8,128)(2,1)} copy(bf16[80,15,16]{0,2,1:T(8,128)(2,1)S(1)} %bitcast.3) | data formatting | bytes 76800

commit v13 on v7

--- a/solution.py
+++ b/solution.py
@@ -380,7 +380,6 @@
             extra_core_send(b)
 
     core_reduce(1, 0)
-    extra_step(extra_core_reduce)
     here = both + pool_get(10) + pool_get(11) + pool_get(12)
     poolsrc[2] = here
     pool_send(poolsrc.at[2], 3, at_z(4))
@@ -390,6 +389,7 @@
     core_send(2, 0)
     compute(1, 3, 5)
     core_send(1, 1)
+    extra_step(extra_core_reduce)
     x_half(0, 0)
     x_half(0, 1)
     core_reduce(2, 0)

time: 62.8 us -> 65.2 us (1.038)
  Pallas kernels: 62 us -> 64.5 us
    pallas_call x1, Pallas kernels: 62 us -> 64.5 us  [local(): pl.pallas_call(head_kernel, out_shape=pltpu.VMEM((15, 16, 80), BF16), in_...]
where the time goes in v13:
time: 65.2 us; the launch traced here: 65.1 us
  Pallas kernels  64.5 us (99%)
    pallas_call x1, Pallas kernels, local(): pl.pallas_call(head_kernel, out_shape=pltpu.VMEM((15, 16, 80), BF16), in_...  64.5 us

profile of v13, /device:TPU:1, one launch (start us, length us, event | category | flops | bytes accessed | tf_op | source)
XLA Modules:
  0.0 65.1 jit_solution(6813657272680736139)
XLA Ops:
  0.0 64.5 %aspp_head.1 = bf16[15,16,80]{2,1,0:T(8,128)(2,1)S(1)} custom-call(bf16[15,80,128]{2,1,0:T(8,128)(2,1)} %bitcast.5, bf16[128,256]{1,0:T(8,128)(2,1)} %pw.1, bf16[3,9,128,256]{3,2,1,0:T(8,128)(2,1)} %bitcast.4, bf16[128,256]{1,0:T(8,128)(2,1)} %wpool_h.1, bf16[1280,256]{1,0:T(8,128)(2,1)} %wproj.1, f32[6,256]{1,0:T(8,128)} %gain_h.1, f32[6,256]{1,0:T(8,128)} %shift_h.1), custom_call_target="tpu_custom_call" | custom-call | tf_op jit(solution)/shard_map/aspp_head/pallas_call | solution.py:543
  64.5 0.6 copy.9

commit v14 on v7

--- a/solution.py
+++ b/solution.py
@@ -404,12 +404,12 @@
     x_half(1, 0)
     core_reduce(3, 0)
     core_reduce(2, 1)
+    extra_step(extra_x_reduce)
     three = here + pool_get(3) + pool_get(4)
     pool_send(poolbuf.at[4], 5, at_z(12))
     halo_wait(2)
     compute(3, 3, 5)
     core_send(3, 1)
-    extra_step(extra_x_reduce)
     x_half(2, 0)
     x_half(1, 1)
     x_reduce(1, 0)

time: 62.8 us -> 64.8 us (1.032)
  Pallas kernels: 62 us -> 64.1 us
    pallas_call x1, Pallas kernels: 62 us -> 64.1 us  [local(): pl.pallas_call(head_kernel, out_shape=pltpu.VMEM((15, 16, 80), BF16), in_...]
where the time goes in v14:
time: 64.8 us; the launch traced here: 64.7 us
  Pallas kernels  64.1 us (99%)
    pallas_call x1, Pallas kernels, local(): pl.pallas_call(head_kernel, out_shape=pltpu.VMEM((15, 16, 80), BF16), in_...  64.1 us

profile of v14, /device:TPU:1, one launch (start us, length us, event | category | flops | bytes accessed | tf_op | source)
XLA Modules:
  0.0 64.7 jit_solution(17984003385650112253)
XLA Ops:
  0.0 64.1 %aspp_head.1 = bf16[15,16,80]{2,1,0:T(8,128)(2,1)S(1)} custom-call(bf16[15,80,128]{2,1,0:T(8,128)(2,1)} %bitcast.5, bf16[128,256]{1,0:T(8,128)(2,1)} %pw.1, bf16[3,9,128,256]{3,2,1,0:T(8,128)(2,1)} %bitcast.4, bf16[128,256]{1,0:T(8,128)(2,1)} %wpool_h.1, bf16[1280,256]{1,0:T(8,128)(2,1)} %wproj.1, f32[6,256]{1,0:T(8,128)} %gain_h.1, f32[6,256]{1,0:T(8,128)} %shift_h.1), custom_call_target="tpu_custom_call" | custom-call | tf_op jit(solution)/shard_map/aspp_head/pallas_call | solution.py:543
  64.1 0.6 copy.9
